TPU v7x, 512 devices: a whole 4x4x16 slice. The times are simulated.
512 devices in a mesh: sector: 16 (over y, x), dom: 32 (over z, core).
Axes of the slice: x: 4, y: 4, z: 16, core: 2. Of those that a mesh axis runs over, the one named last changes fastest.
Arguments:
- strain_map: float32 [36, 131072], P(None, ('sector', 'dom')), may hold values from -1.75 to 1.75
- corner_nodes: int32 [4, 131072], P(None, ('sector', 'dom')), may hold values from 0 to 10239, as said below
- counts: int32 [512], P(('sector', 'dom')), may hold values from 64 to 256, as said below
- seam_nodes: int32 [16, 2048], P('sector'), may hold values from 0 to 8191
- velocity: float32 [3, 131072], P(None, ('sector', 'dom')), may hold values from -6 to 6
- dual_state: float32 [3, 131072], P(None, ('sector', 'dom')), may hold values from -6 to 6
- nodal_load: float32 [3, 131072], P(None, ('sector', 'dom')), may hold values from -6 to 6
- mobility: float32 [131072], P(('sector', 'dom')), may hold values from 0.1 to 0.5
- past_dual: float32 [8, 3, 131072], P(None, None, ('sector', 'dom')), may hold values from -6 to 6
- past_dual_gap: float32 [8, 3, 131072], P(None, None, ('sector', 'dom')), may hold values from -12 to 12
- past_velocity: float32 [8, 3, 131072], P(None, None, ('sector', 'dom')), may hold values from -6 to 6
- past_velocity_gap: float32 [8, 3, 131072], P(None, None, ('sector', 'dom')), may hold values from -12 to 12
Outputs:
- new_velocity: float32 [3, 131072], P(None, ('sector', 'dom'))
- new_dual: float32 [3, 131072], P(None, ('sector', 'dom'))
Inputs may be any that keep to these rules, and one draw needn't show every extreme that they name: `counts`: each block has between 64 and 256 live elements; some block is full and some has exactly the least. `corner_nodes`: an element of block d of a sector (d = its slot's block index along dom) names either a seam position (8192 and up) or a node from d * 256 - 32 to (d + 1) * 256 + 31, within 0 to 8191; both ends of that range are named in every draw where they exist.
All inputs are finite; a program needn't handle non-finite values.
Results may differ from a plain program's by a relative error of at most 0.0003.
Values sent between devices are 32-bit elements; how exact they have to be, the bound alone decides.
A program may use at most 64 MiB of HBM per device.

v0:
```python
import jax
import jax.numpy as jnp
from jax import lax
from jax.sharding import PartitionSpec as P

ITERS = 2


def shifted(value, axis, by):
    size = lax.axis_size(axis)
    return lax.ppermute(value, axis, [(i, (i + by) % size) for i in range(size)])


def project_cone(trial):
    center = 0.5 * (trial[0] + trial[1])
    spread = 0.5 * (trial[0] - trial[1])
    shear = trial[2]
    radius = jnp.sqrt(spread * spread + shear * shear)
    upper = center + radius
    lower = center - radius
    iso_part = 0.5 * (jnp.maximum(upper, 0.0) + jnp.maximum(lower, 0.0))
    factor = jnp.clip((center + radius) / (2.0 * jnp.maximum(radius, 0.05)), 0.0, 1.0)
    return jnp.stack([iso_part + factor * spread, iso_part - factor * spread, factor * shear])


def panel_gram(left_w, left_u):
    highest = lax.Precision.HIGHEST
    return jnp.einsum("iab,jab->ij", left_w, left_w, precision=highest) + jnp.einsum(
        "iab,jab->ij", left_u, left_u, precision=highest
    )


def panel_vector(left_w, left_u, right_w, right_u):
    highest = lax.Precision.HIGHEST
    return jnp.einsum("iab,ab->i", left_w, right_w, precision=highest) + jnp.einsum(
        "iab,ab->i", left_u, right_u, precision=highest
    )


def seam_pull(seam_values):
    return shifted(seam_values, "sector", -1)


def seam_push(seam_part):
    return shifted(seam_part, "sector", 1)


def per_device(
    strain_map,
    corner_nodes,
    counts,
    seam_nodes,
    velocity,
    dual_state,
    nodal_load,
    mobility,
    past_dual,
    past_dual_gap,
    past_velocity,
    past_velocity_gap,
):
    highest = lax.Precision.HIGHEST
    elem_count = strain_map.shape[1]
    own_nodes = velocity.shape[1]
    sector_nodes = own_nodes * lax.axis_size("dom")
    seam_list = seam_nodes[0]
    seam_count = seam_list.shape[0]
    slot_index = jnp.arange(elem_count, dtype=jnp.int32)
    alive_mask = (slot_index < counts[0]).astype(jnp.float32)
    flat_nodes = corner_nodes.reshape(-1)
    strain_blocks = strain_map.reshape(3, 4, 3, elem_count)
    depth = past_dual.shape[0]
    dual = dual_state
    dual_prev = dual
    sector_speed, load_full, mobility_full = (
        lax.all_gather(velocity, "dom", axis=1, tiled=True),
        lax.all_gather(nodal_load, "dom", axis=1, tiled=True),
        lax.all_gather(mobility, "dom", axis=0, tiled=True),
    )
    full_prev = sector_speed
    for sweep in range(ITERS):
        dual_prev, full_prev = (dual, sector_speed)
        seam_recv = seam_pull(sector_speed[:, seam_list])
        sector_extended = jnp.concatenate([sector_speed, seam_recv], axis=1)
        corner_vel = sector_extended[:, flat_nodes].reshape(3, 4, elem_count).transpose(1, 0, 2)
        rate = jnp.sum(strain_blocks * corner_vel[None], axis=(1, 2))
        trial = rate + dual
        cone = project_cone(trial)
        dual_next = alive_mask * (trial - cone)
        misfit = alive_mask * (rate - cone + dual_next)
        elem_force = jnp.sum(strain_blocks * misfit[:, None, None, :], axis=0)
        spread_force = elem_force.transpose(1, 0, 2).reshape(3, -1)
        partial_value = (
            jnp.zeros((3, sector_nodes + seam_count), jnp.float32)
            .at[:, flat_nodes]
            .add(spread_force)
        )
        seam_back = seam_push(partial_value[:, sector_nodes:])
        own_forces = partial_value[:, :sector_nodes].at[:, seam_list].add(seam_back)
        dual, own_forces = (dual_next, own_forces)
        forces = lax.psum(own_forces, "dom")
        sector_speed = sector_speed - mobility_full[None, :] * (forces - load_full)
    start = lax.axis_index("dom") * own_nodes
    speed = lax.dynamic_slice_in_dim(sector_speed, start, own_nodes, 1)
    speed_prev = lax.dynamic_slice_in_dim(full_prev, start, own_nodes, 1)
    res_w = dual - dual_prev
    res_u = speed - speed_prev
    gap_w = res_w[None] - past_dual_gap
    gap_u = res_u[None] - past_velocity_gap
    gram_local = panel_gram(gap_w, gap_u)
    rhs_local = panel_vector(gap_w, gap_u, res_w, res_u)
    gram, rhs = lax.psum((gram_local, rhs_local), ("sector", "dom"))
    ridge_term = 0.0001 * jnp.trace(gram) / depth
    factor = jnp.linalg.cholesky(gram + ridge_term * jnp.eye(depth, dtype=jnp.float32))
    coeffs = jax.scipy.linalg.cho_solve((factor, True), rhs)
    new_dual = dual - jnp.einsum(
        "i,iab->ab", coeffs, dual[None] - past_dual - past_dual_gap, precision=highest
    )
    new_velocity = speed - jnp.einsum(
        "i,iab->ab", coeffs, speed[None] - past_velocity - past_velocity_gap, precision=highest
    )
    return (new_velocity, new_dual)


def solution(mesh):
    in_specs = (
        P(None, ("sector", "dom")),
        P(None, ("sector", "dom")),
        P(("sector", "dom")),
        P("sector", None),
        P(None, ("sector", "dom")),
        P(None, ("sector", "dom")),
        P(None, ("sector", "dom")),
        P(("sector", "dom")),
        P(None, None, ("sector", "dom")),
        P(None, None, ("sector", "dom")),
        P(None, None, ("sector", "dom")),
        P(None, None, ("sector", "dom")),
    )
    out_specs = (P(None, ("sector", "dom")), P(None, ("sector", "dom")))
    return jax.shard_map(
        per_device, mesh=mesh, in_specs=in_specs, out_specs=out_specs, check_vma=False
    )
```

profile of v0, /device:TPU:1, one launch (start us, length us, event | category | flops | bytes accessed | tf_op | source)
XLA Modules:
  0.0 752.0 jit_solution(2183255588971911580)
XLA Ops:
  8.8 52.7 %all_gather.9 = f32[3,8192]{0,1:T(8,128)} all-gather(f32[3,256]{0,1:T(8,128)S(1)} %copy.92), channel_id=1, replica_groups=mesh['sector'=16,'dom'=32] {'dom'}, dimensions={1}, use_global_device_ids=true | all-gather | bytes 101376 | tf_op jit(solution)/shard_map/all_gather | solution.py:76
  61.5 7.6 %gather_fusion = f32[2048,3]{1,0:T(8,128)S(1)} fusion(f32[3,8192]{0,1:T(8,128)} %all_gather.9, s32[2048]{0:T(1024)S(1)} %broadcast_clamp_fusion), kind=kCustom, calls=%fused_computation | custom fusion | bytes 57344 | tf_op jit(solution)/shard_map/gather | solution.py:83
  69.5 6.8 collective-permute-start
  77.7 5.1 pad_maximum_fusion
  82.8 5.3 gather_fusion.1
  88.7 8.6 %scatter_custom_fusion = f32[3,10240]{0,1:T(8,128)} fusion(s32[1024]{0:T(1024)S(1)} %bitcast.97, f32[1024,3]{1,0:T(8,128)S(1)} %copy.96, f32[]{:T(128)} %constant.71.clone.1), kind=kCustom, calls=%fused_computation.13 | custom fusion | flops 3072 | bytes 122884 | tf_op jit(solution)/shard_map/scatter-add | solution.py:96
  98.9 1.9 collective-permute-start.1
  100.9 4.4 slice.73
  105.3 1.9 collective-permute-done.1
  107.6 14.4 %scatter_fusion = f32[3,8192]{0,1:T(8,128)} fusion(f32[3,8192]{0,1:T(8,128)} %slice.73, s32[2048]{0:T(1024)S(1)} %bitcast.89, f32[2048,3]{1,0:T(8,128)S(1)} %copy.98), kind=kCustom, calls=%fused_computation.5 | custom fusion | flops 6144 | bytes 81920 | tf_op jit(solution)/shard_map/scatter-add | solution.py:99
  122.1 28.8 %all-gather = f32[32,1,256]{2,1,0:T(1,128)S(1)} all-gather(f32[1,1,256]{2,1,0:T(1,128)S(1)} %bitcast.102), channel_id=1, replica_groups=mesh['sector'=16,'dom'=32] {'dom'}, dimensions={0}, use_global_device_ids=true | all-gather | bytes 33792 | tf_op jit(solution)/shard_map/all_gather | solution.py:78
  151.0 50.1 %all_gather.11 = f32[3,8192]{0,1:T(8,128)} all-gather(f32[3,256]{0,1:T(8,128)S(1)} %copy.99), channel_id=1, replica_groups=mesh['sector'=16,'dom'=32] {'dom'}, dimensions={1}, use_global_device_ids=true | all-gather | bytes 101376 | tf_op jit(solution)/shard_map/all_gather | solution.py:77
  201.2 141.6 %all-reduce.4.cloned.1.call-done = f32[3,8192]{0,1:T(8,128)} async-done(((f32[3,8192]{0,1:T(8,128)}), f32[3,8192]{0,1:T(8,128)}) %all-reduce.4.cloned.1.call-update) | async-done | bytes 98320 | tf_op jit(solution)/shard_map/psum | solution.py:101
  342.7 7.1 multiply_subtract_fusion
  349.8 7.6 %gather_fusion.2 = f32[2048,3]{1,0:T(8,128)S(1)} fusion(f32[3,8192]{0,1:T(8,128)} %multiply_subtract_fusion, s32[2048]{0:T(1024)S(1)} %broadcast_clamp_fusion), kind=kCustom, calls=%fused_computation.2 | custom fusion | bytes 57344 | tf_op jit(solution)/shard_map/gather | solution.py:83
  357.8 6.7 collective-permute-start.2
  365.7 5.1 pad_maximum_fusion.1
  370.8 5.3 gather_fusion.3
  376.7 8.6 %scatter_custom_fusion.2 = f32[3,10240]{0,1:T(8,128)} fusion(s32[1024]{0:T(1024)S(1)} %bitcast.98, f32[1024,3]{1,0:T(8,128)S(1)} %copy.103, f32[]{:T(128)} %constant.71.clone.1), kind=kCustom, calls=%fused_computation.11 | custom fusion | flops 3072 | bytes 122884 | tf_op jit(solution)/shard_map/scatter-add | solution.py:96
  388.9 4.4 slice.78
  393.3 1.9 collective-permute-done.3
  395.6 14.4 %scatter_fusion.1 = f32[3,8192]{0,1:T(8,128)} fusion(f32[3,8192]{0,1:T(8,128)} %slice.78, s32[2048]{0:T(1024)S(1)} %bitcast.90, f32[2048,3]{1,0:T(8,128)S(1)} %copy.105), kind=kCustom, calls=%fused_computation.7 | custom fusion | flops 6144 | bytes 81920 | tf_op jit(solution)/shard_map/scatter-add | solution.py:99
  410.1 221.2 %all-reduce.6.cloned.1.call-done = f32[3,8192]{0,1:T(8,128)} async-done(((f32[3,8192]{0,1:T(8,128)}), f32[3,8192]{0,1:T(8,128)}) %all-reduce.6.cloned.1.call-update) | async-done | bytes 98320 | tf_op jit(solution)/shard_map/psum | solution.py:101
  633.3 105.5 %all-reduce = (f32[8,8]{0,1:T(8,128)S(1)}, f32[8]{0:T(128)S(1)}) all-reduce(f32[8,8]{0,1:T(8,128)S(1)} %fusion.4, f32[8]{0:T(128)S(1)} %fusion.5), channel_id=1, replica_groups=mesh['sector'=16,'dom'=32] {'sector','dom'}, use_global_device_ids=true, to_apply=%region_10.11 | all-reduce | flops 72 | bytes 576 | tf_op jit(solution)/shard_map/psum | solution.py:112
  (89 shorter events, 19.0 us)
Async XLA Ops:
  7.2 69.1 %copy-start.7 = (s32[4,256]{1,0:T(4,128)S(1)}, s32[4,256]{1,0:T(4,128)}, u32[]{:S(2)}) copy-start(s32[4,256]{1,0:T(4,128)} %param.13) | copy-start | bytes 12292
  7.2 69.8 %copy-start.2 = (f32[36,256]{1,0:T(8,128)S(1)}, f32[36,256]{1,0:T(8,128)}, u32[]{:S(2)}) copy-start(f32[36,256]{1,0:T(8,128)} %param.12) | copy-start | bytes 110596
  7.2 335.5 %all-reduce.4.cloned.1.call-start = ((), (), s32[]{:S(2)}) async-start(), calls=%async_computation | async-start | bytes 8388608 | tf_op jit(solution)/shard_map/psum | solution.py:101
  69.5 7.8 %collective-permute-start = (f32[3,2048]{1,0:T(4,128)S(1)}, f32[3,2048]{1,0:T(4,128)S(1)}, u32[]{:S(2)}, u32[]{:S(2)}) collective-permute-start(f32[3,2048]{1,0:T(4,128)S(1)} %copy.93), channel_id=1, source_target_pairs={{0,480},{32,0},{64,32},{96,64},{128,96},{160,128},{192,160},{224,1... | collective-permute-start | bytes 73736 | tf_op jit(solution)/shard_map/ppermute | solution.py:11
  77.7 10.7 %copy-start.5 = (f32[3,256]{1,0:T(4,128)S(1)}, f32[3,256]{1,0:T(4,128)}, u32[]{:S(2)}) copy-start(f32[3,256]{1,0:T(4,128)} %param.17) | copy-start | bytes 9220
  98.9 8.3 %collective-permute-start.1 = (f32[3,2048]{1,0:T(4,128)S(1)}, f32[3,2048]{1,0:T(4,128)S(1)}, u32[]{:S(2)}, u32[]{:S(2)}) collective-permute-start(f32[3,2048]{1,0:T(4,128)S(1)} %copy.97), channel_id=1, source_target_pairs={{0,32},{32,64},{64,96},{96,128},{128,160},{160,192},{192,224},{224... | collective-permute-start | bytes 73736 | tf_op jit(solution)/shard_map/ppermute | solution.py:11
  105.3 16.8 %copy-start.8 = (f32[256]{0:T(256)S(1)}, f32[256]{0:T(256)}, u32[]{:S(2)}) copy-start(f32[256]{0:T(256)} %param.19) | copy-start | bytes 3076
  105.3 45.6 %copy-start.6 = (f32[3,256]{1,0:T(4,128)S(1)}, f32[3,256]{1,0:T(4,128)}, u32[]{:S(2)}) copy-start(f32[3,256]{1,0:T(4,128)} %param.18) | copy-start | bytes 9220
  122.0 509.3 %all-reduce.6.cloned.1.call-start = ((), (), s32[]{:S(2)}) async-start(), calls=%async_computation.1 | async-start | bytes 8388608 | tf_op jit(solution)/shard_map/psum | solution.py:101
  357.8 7.5 collective-permute-start.2
  387.0 8.3 %collective-permute-start.3 = (f32[3,2048]{1,0:T(4,128)S(1)}, f32[3,2048]{1,0:T(4,128)S(1)}, u32[]{:S(2)}, u32[]{:S(2)}) collective-permute-start(f32[3,2048]{1,0:T(4,128)S(1)} %copy.104), channel_id=1, source_target_pairs={{0,32},{32,64},{64,96},{96,128},{128,160},{160,192},{192,224},{224... | collective-permute-start | bytes 73736 | tf_op jit(solution)/shard_map/ppermute | solution.py:11
  393.3 239.4 %copy-start.1 = (f32[8,3,256]{2,0,1:T(8,128)S(1)}, f32[8,3,256]{2,0,1:T(8,128)}, u32[]{:S(2)}) copy-start(f32[8,3,256]{2,0,1:T(8,128)} %param.23) | copy-start | bytes 73732
  393.3 239.7 %copy-start = (f32[8,3,256]{2,0,1:T(8,128)S(1)}, f32[8,3,256]{2,0,1:T(8,128)}, u32[]{:S(2)}) copy-start(f32[8,3,256]{2,0,1:T(8,128)} %param.21) | copy-start | bytes 73732
  393.3 350.0 %copy-start.3 = (f32[8,3,256]{2,0,1:T(8,128)S(1)}, f32[8,3,256]{2,0,1:T(8,128)}, u32[]{:S(2)}) copy-start(f32[8,3,256]{2,0,1:T(8,128)} %param.20) | copy-start | bytes 73732
  393.3 350.9 %copy-start.4 = (f32[8,3,256]{2,0,1:T(8,128)S(1)}, f32[8,3,256]{2,0,1:T(8,128)}, u32[]{:S(2)}) copy-start(f32[8,3,256]{2,0,1:T(8,128)} %param.22) | copy-start | bytes 73732
Sparse Core Ops, SparseCore 0:
  122.1 220.5 all-reduce.3
  410.2 221.1 all-reduce.5
where the time goes:
time: 753 us; the launch traced here: 752 us
  waiting for transfers between devices  368 us (49%)
  blocking collectives  237 us (31%)
  other arithmetic  69.6 us (9%)
  local copies, waits for them, and re-layouts  43.1 us (6%)
  starting transfers between devices  17.4 us (2%)
  between operations  15.7 us (2%)
    psum x2, waiting for transfers between devices, per_device(): forces = lax.psum(own_forces, 'dom')  363 us
    psum x1, blocking collectives, per_device(): gram, rhs = lax.psum((gram_local, rhs_local), ('sector', 'dom'))  105 us
    all_gather x1, blocking collectives, per_device(): lax.all_gather(velocity, 'dom', axis=1, tiled=True)  52.7 us
    all_gather x1, blocking collectives, per_device(): lax.all_gather(nodal_load, 'dom', axis=1, tiled=True)  50.1 us
    scatter-add x2, other arithmetic, per_device(): own_forces = partial_value[:, :sector_nodes].at[:, seam_list].add(seam_back)  28.9 us
    all_gather x1, blocking collectives, per_device(): lax.all_gather(mobility, 'dom', axis=0, tiled=True)  28.8 us
    ppermute x4, starting transfers between devices, shifted(): lax.ppermute(value, axis, [(i, (i + by) % size) for i in range(size)])  17.4 us
    scatter-add x2, other arithmetic, per_device(): partial_value = jnp.zeros((3, sector_nodes + seam_count), jnp.float32).at...  17.2 us
  transfers between devices with their start and end apart: 6, of which 6 were waited for; matrix products, arithmetic and copies ran while one was open for 1% of the time, Pallas kernels for 0%

commit v1 on v0

v1 whole, which is shorter than its diff:
```python
import functools

import jax
import jax.numpy as jnp
from jax import lax
from jax.experimental import pallas as pl
from jax.experimental.pallas import tpu as pltpu
from jax.sharding import PartitionSpec as P

MESH = pl.DeviceIdType.MESH
ITERS = 2
LANES = 128


def row_bcast(x, r):
    return jnp.broadcast_to(x[r : r + 1, :], (8, LANES))


def lane_take(row, index):
    return jnp.take_along_axis(row, index, axis=1, mode="promise_in_bounds")


def sum_corners(x, iota_row):
    odd = lax.rem(iota_row, 2) == 1
    x = x + jnp.where(odd, pltpu.roll(x, 1, 0), pltpu.roll(x, 7, 0))
    high = lax.rem(iota_row, 4) >= 2
    return x + jnp.where(high, pltpu.roll(x, 2, 0), pltpu.roll(x, 6, 0))


def project_cone(a, b, shear):
    center = 0.5 * (a + b)
    spread = 0.5 * (a - b)
    radius = jnp.sqrt(spread * spread + shear * shear)
    upper = center + radius
    lower = center - radius
    iso_part = 0.5 * (jnp.maximum(upper, 0.0) + jnp.maximum(lower, 0.0))
    factor = jnp.clip(upper / (2.0 * jnp.maximum(radius, 0.05)), 0.0, 1.0)
    return iso_part + factor * spread, iso_part - factor * spread, factor * shear


def kernel(
    sectors,
    doms,
    strain,
    corner,
    counts,
    seam,
    velocity,
    dual,
    load,
    mobility,
    past_dual,
    past_dual_gap,
    past_velocity,
    past_velocity_gap,
    new_velocity,
    new_dual,
    speed,
    load6,
    mob6,
    strain_r,
    seam_in,
    speed_in,
    edge_in,
    force,
    force_in,
    push_in,
    onehot,
    gram_out,
    gram_in,
    total_out,
    total_in,
    send_sem,
    recv_sem,
):
    sec = lax.axis_index("sector")
    dom = lax.axis_index("dom")
    prev_sec = lax.rem(sec + sectors - 1, sectors)
    next_sec = lax.rem(sec + 1, sectors)
    left = lax.rem(dom + doms - 1, doms)
    right = lax.rem(dom + 1, doms)

    def copy(src, dst, sem, s, d):
        return pltpu.make_async_remote_copy(
            src_ref=src,
            dst_ref=dst,
            send_sem=send_sem.at[sem],
            recv_sem=recv_sem.at[sem],
            device_id=(s, d),
            device_id_type=MESH,
        )

    def far_first(k):
        step = (k + 1) // 2
        return lax.rem(dom + doms // 2 + jnp.where(lax.rem(k, 2) == 1, doms - step, step), doms)

    barrier = pltpu.get_barrier_semaphore()

    def signal(s, d):
        pl.semaphore_signal(barrier, inc=1, device_id=(s, d), device_id_type=MESH)

    def greet_dom(k, c):
        d = far_first(k)
        signal(prev_sec, d)
        signal(next_sec, d)
        return c

    def greet_own(k, c):
        signal(sec, far_first(k))
        return c

    def greet_sec(o, c):
        signal(lax.rem(sec + o, sectors), dom)
        return c

    lax.fori_loop(0, doms, greet_dom, 0)
    lax.fori_loop(0, doms - 1, greet_own, 0)
    lax.fori_loop(2, sectors - 1, greet_sec, 0)

    iota_row = lax.broadcasted_iota(jnp.int32, (8, LANES), 0)
    iota_lane = lax.broadcasted_iota(jnp.int32, (8, LANES), 1)

    speed[...] = jnp.zeros_like(speed)
    load6[...] = jnp.zeros_like(load6)
    for j in range(3):
        for h in range(2):
            r, cols = 2 * j + h, pl.ds(LANES * h, LANES)
            speed[0, r : r + 1, :] = velocity[j : j + 1, cols]
            load6[r : r + 1, :] = load[j : j + 1, cols]
    mob6[...] = jnp.where(
        lax.rem(iota_row, 2) == 0,
        jnp.broadcast_to(mobility[0:1, :], (8, LANES)),
        jnp.broadcast_to(mobility[1:2, :], (8, LANES)),
    )

    pl.semaphore_wait(barrier, 2 * doms + (doms - 1) + (sectors - 3))

    six = pl.ds(0, 6)

    def send_speed(it):
        def body(k, c):
            d = far_first(k)
            copy(speed.at[it, six], speed_in.at[it, dom, six], 8 * it + 0, prev_sec, d).start()
            return c

        copy(speed.at[it, six], edge_in.at[it, 0, six], 8 * it + 1, sec, right).start()
        copy(speed.at[it, six], edge_in.at[it, 1, six], 8 * it + 2, sec, left).start()
        lax.fori_loop(0, doms, body, 0)

    def wait_speed(it):
        copy(speed.at[it, six], edge_in.at[it, 0, six], 8 * it + 1, sec, right).wait()
        copy(speed.at[it, six], edge_in.at[it, 1, six], 8 * it + 2, sec, left).wait()
        block = speed_in.at[it, :, six]
        copy(block, block, 8 * it + 0, prev_sec, dom).wait()

    def send_force(it):
        def body(k, c):
            d = far_first(k)
            copy(force.at[it, 2 + d, six], force_in.at[it, dom, six], 8 * it + 3, next_sec, d).start()
            return c

        copy(force.at[it, 0, six], push_in.at[it, 1, six], 8 * it + 4, sec, left).start()
        copy(force.at[it, 1, six], push_in.at[it, 0, six], 8 * it + 5, sec, right).start()
        lax.fori_loop(0, doms, body, 0)

    def wait_force(it):
        copy(force.at[it, 0, six], push_in.at[it, 1, six], 8 * it + 4, sec, left).wait()
        copy(force.at[it, 1, six], push_in.at[it, 0, six], 8 * it + 5, sec, right).wait()
        block = force_in.at[it, :, six]
        copy(block, block, 8 * it + 3, next_sec, dom).wait()

    seam_copy = copy(seam, seam_in, 6, prev_sec, dom)
    seam_copy.start()
    send_speed(0)

    for c in range(3):
        for j in range(3):
            for k in range(4):
                r = 12 * c + 3 * k + j
                for h in range(2):
                    strain_r[3 * c + j, 4 * h + k : 4 * h + k + 1, :] = strain[r : r + 1, pl.ds(LANES * h, LANES)]
    nodes = jnp.concatenate([corner[:, 0:LANES], corner[:, LANES : 2 * LANES]], axis=0)
    slot = LANES * (iota_row // 4) + iota_lane
    alive = jnp.where(slot < counts[0], 1.0, 0.0)
    dual_prev = [
        jnp.where(
            iota_row < 4,
            jnp.broadcast_to(dual[c : c + 1, 0:LANES], (8, LANES)),
            jnp.broadcast_to(dual[c : c + 1, LANES : 2 * LANES], (8, LANES)),
        )
        for c in range(3)
    ]

    sector_nodes = doms * 2 * LANES
    seam_copy.wait()
    position = nodes - sector_nodes
    place = jnp.bitwise_and(position, LANES - 1)
    place_row = jnp.right_shift(position, 7)
    seam_node = jnp.zeros((8, LANES), jnp.int32)
    for r in range(seam.shape[1] // LANES):
        row = jnp.broadcast_to(seam_in[0:1, LANES * r : LANES * (r + 1)], (8, LANES))
        seam_node = jnp.where(place_row == r, lane_take(row, place), seam_node)
    is_seam = position >= 0
    key = jnp.where(is_seam, 4 + jnp.right_shift(seam_node, 7), jnp.right_shift(nodes, 7) - 2 * dom + 1)
    low = jnp.bitwise_and(jnp.where(is_seam, seam_node, nodes), LANES - 1)

    lane_is = lax.broadcasted_iota(jnp.int32, (LANES, LANES), 0)
    for t in range(8):
        hit = lane_is == jnp.broadcast_to(low[t : t + 1, :], (LANES, LANES))
        onehot[:, LANES * t : LANES * (t + 1)] = jnp.where(hit, 1.0, 0.0).astype(jnp.bfloat16)

    def elements(it, dual_now):
        def look(table, row_key, acc, h):
            out = []
            for j in range(3):
                row = jnp.broadcast_to(table[2 * j + h : 2 * j + h + 1, :], (8, LANES))
                out.append(jnp.where(key == row_key, lane_take(row, low), acc[j]))
            return out

        acc = [jnp.zeros((8, LANES), jnp.float32)] * 3
        acc = look(edge_in.at[it, 0], 0, acc, 1)
        acc = look(speed.at[it], 1, acc, 0)
        acc = look(speed.at[it], 2, acc, 1)
        acc = look(edge_in.at[it, 1], 3, acc, 0)

        def body(b, acc):
            acc = look(speed_in.at[it, b], 4 + 2 * b, acc, 0)
            return tuple(look(speed_in.at[it, b], 5 + 2 * b, acc, 1))

        acc = lax.fori_loop(0, doms, body, tuple(acc))
        rate = []
        for c in range(3):
            part = strain_r[3 * c] * acc[0] + strain_r[3 * c + 1] * acc[1] + strain_r[3 * c + 2] * acc[2]
            rate.append(sum_corners(part, iota_row))
        trial = [rate[c] + dual_now[c] for c in range(3)]
        cone = project_cone(*trial)
        dual_next = [alive * (trial[c] - cone[c]) for c in range(3)]
        misfit = [alive * (rate[c] - cone[c] + dual_next[c]) for c in range(3)]
        push = [
            strain_r[j] * misfit[0] + strain_r[3 + j] * misfit[1] + strain_r[6 + j] * misfit[2] for j in range(3)
        ]
        return dual_next, push

    def spread(it, push):
        wanted, split = [], [[], [], []]
        for t in range(8):
            value = jnp.where(iota_row < 2, row_bcast(push[0], t), row_bcast(push[1], t))
            value = jnp.where(iota_row < 4, value, row_bcast(push[2], t))
            value = jnp.where(iota_row < 6, value, 0.0)
            wanted.append(row_bcast(key, t) - jnp.bitwise_and(iota_row, 1))
            for s in range(3):
                piece = value.astype(jnp.bfloat16).astype(jnp.float32)
                split[s].append(piece)
                value = value - piece
        wanted = jnp.concatenate(wanted, axis=1)
        split = [jnp.concatenate(p, axis=1) for p in split]

        def body(q, c):
            total = jnp.zeros((16, LANES), jnp.float32)
            for s in range(3):
                pair = [jnp.where(wanted == 4 * q + 2 * i, split[s], 0.0) for i in range(2)]
                left_side = jnp.concatenate(pair, axis=0).astype(jnp.bfloat16)
                total = total + lax.dot_general(
                    left_side,
                    onehot[...],
                    (((1,), (1,)), ((), ())),
                    preferred_element_type=jnp.float32,
                )
            force[it, 2 * q] = total[0:8]
            force[it, 2 * q + 1] = total[8:16]
            return c

        lax.fori_loop(0, (doms + 2) // 2, body, 0)

    def next_speed(it):
        even = lax.rem(iota_row, 2) == 0
        own = jnp.where(
            even,
            pltpu.roll(force[it, 0] + jnp.where(iota_row < 6, push_in[it, 0], 0.0), 7, 0),
            pltpu.roll(force[it, 1] + jnp.where(iota_row < 6, push_in[it, 1], 0.0), 1, 0),
        )

        def body(b, acc):
            return acc + force_in[it, b]

        own = lax.fori_loop(0, doms, body, own)
        step = speed[it] - mob6[...] * (own - load6[...])
        return jnp.where(iota_row < 6, step, 0.0)

    wait_speed(0)
    dual_one, push = elements(0, dual_prev)
    spread(0, push)
    send_force(0)
    wait_force(0)
    speed[1] = next_speed(0)
    send_speed(1)
    wait_speed(1)
    dual_two, push = elements(1, dual_one)
    spread(1, push)
    send_force(1)

    def by_history(ref, j, h):
        return ref[:, j, pl.ds(LANES * h, LANES)]

    depth = 8
    acc = [jnp.zeros((8, LANES), jnp.float32)] * (depth + 1)

    def add_gram(acc, res_row, past):
        res_b = jnp.broadcast_to(res_row, (8, LANES))
        gap = res_b - past
        acc = [acc[i] + gap * row_bcast(gap, i) for i in range(depth)] + [acc[depth] + gap * res_b]
        return acc

    for c in range(3):
        res = dual_two[c] - dual_one[c]
        for h in range(2):
            acc = add_gram(acc, res[4 * h : 4 * h + 1, :], by_history(past_dual_gap, c, h))

    wait_force(1)
    speed_one = speed[1]
    speed_two = next_speed(1)
    res = speed_two - speed_one
    for j in range(3):
        for h in range(2):
            r = 2 * j + h
            acc = add_gram(acc, res[r : r + 1, :], by_history(past_velocity_gap, j, h))
    packed = jnp.zeros((8, LANES), jnp.float32)
    for i in range(depth + 1):
        packed = jnp.where(iota_lane == i, jnp.sum(acc[i], axis=1, keepdims=True), packed)

    def fold(x):
        out = x[0:1, :]
        for l in range(1, 8):
            out = out + pltpu.roll(x[l : l + 1, :], 16 * l, 1)
        return out

    gram_out[0] = fold(packed)

    def send_gram(k, c):
        copy(gram_out.at[0], gram_in.at[k], 7, sec, far_first(k)).start()
        return c

    lax.fori_loop(0, doms - 1, send_gram, 0)
    block = gram_in.at[pl.ds(0, doms - 1)]
    copy(block, block, 7, sec, dom).wait()

    def add_in(o, acc):
        return acc + gram_in[o]

    total = lax.fori_loop(0, doms - 1, add_in, gram_out[0])
    total_out[0] = total

    def send_total(o, c):
        copy(total_out.at[0], total_in.at[o], 14, lax.rem(sec + o, sectors), dom).start()
        return c

    lax.fori_loop(1, sectors, send_total, 0)
    block = total_in.at[pl.ds(1, sectors - 1)]
    copy(block, block, 14, sec, dom).wait()

    def add_total(o, acc):
        return acc + total_in[o]

    total = lax.fori_loop(1, sectors, add_total, total)

    system = jnp.zeros((8, LANES), jnp.float32)
    for l in range(8):
        row = total if l == 0 else pltpu.roll(total, LANES - 16 * l, 1)
        system = jnp.where(iota_row == l, jnp.broadcast_to(row, (8, LANES)), system)

    diagonal = iota_row == iota_lane
    trace = jnp.sum(jnp.where(diagonal, system, 0.0), axis=1, keepdims=True)
    trace = jnp.sum(trace, axis=0, keepdims=True)
    ridge = jnp.broadcast_to(0.0001 * trace / depth, (8, LANES))
    system = jnp.where(diagonal, system + ridge, system)
    for k in range(depth):
        pivot_row = row_bcast(system, k)
        pivot_row = pivot_row / jnp.broadcast_to(pivot_row[:, k : k + 1], (8, LANES))
        column = jnp.broadcast_to(system[:, k : k + 1], (8, LANES))
        system = jnp.where(iota_row == k, pivot_row, system - column * pivot_row)
    coeffs = jnp.broadcast_to(system[:, depth : depth + 1], (8, LANES))

    def mixed(now_row, past, past_gap):
        now = jnp.broadcast_to(now_row, (8, LANES))
        return now_row - jnp.sum(coeffs * (now - past - past_gap), axis=0, keepdims=True)

    for j in range(3):
        for h in range(2):
            r, cols = 2 * j + h, pl.ds(LANES * h, LANES)
            new_velocity[j : j + 1, cols] = mixed(
                speed_two[r : r + 1, :], by_history(past_velocity, j, h), by_history(past_velocity_gap, j, h)
            )
            new_dual[j : j + 1, cols] = mixed(
                dual_two[j][4 * h : 4 * h + 1, :], by_history(past_dual, j, h), by_history(past_dual_gap, j, h)
            )


def per_device(
    strain_map,
    corner_nodes,
    counts,
    seam_nodes,
    velocity,
    dual_state,
    nodal_load,
    mobility,
    past_dual,
    past_dual_gap,
    past_velocity,
    past_velocity_gap,
):
    sectors, doms = lax.axis_size("sector"), lax.axis_size("dom")
    out = jax.ShapeDtypeStruct(velocity.shape, jnp.float32)
    vmem = pl.BlockSpec(memory_space=pltpu.VMEM)
    smem = pl.BlockSpec(memory_space=pltpu.SMEM)
    f32 = jnp.float32
    return pl.pallas_call(
        functools.partial(kernel, sectors, doms),
        out_shape=(out, out),
        in_specs=[vmem, vmem, smem] + [vmem] * 9,
        out_specs=(vmem, vmem),
        scratch_shapes=[
            pltpu.VMEM((2, 8, LANES), f32),
            pltpu.VMEM((8, LANES), f32),
            pltpu.VMEM((8, LANES), f32),
            pltpu.VMEM((9, 8, LANES), f32),
            pltpu.VMEM(seam_nodes.shape, jnp.int32),
            pltpu.VMEM((2, doms, 8, LANES), f32),
            pltpu.VMEM((2, 2, 8, LANES), f32),
            pltpu.VMEM((2, doms + 2, 8, LANES), f32),
            pltpu.VMEM((2, doms, 8, LANES), f32),
            pltpu.VMEM((2, 2, 8, LANES), f32),
            pltpu.VMEM((LANES, 8 * LANES), jnp.bfloat16),
            pltpu.VMEM((1, 1, LANES), f32),
            pltpu.VMEM((doms, 1, LANES), f32),
            pltpu.VMEM((1, 1, LANES), f32),
            pltpu.VMEM((sectors, 1, LANES), f32),
            pltpu.SemaphoreType.DMA((16,)),
            pltpu.SemaphoreType.DMA((16,)),
        ],
        compiler_params=pltpu.CompilerParams(collective_id=0, has_side_effects=True),
        name="dome",
    )(
        strain_map,
        corner_nodes,
        counts,
        seam_nodes,
        velocity,
        dual_state,
        nodal_load,
        mobility.reshape(2, LANES),
        past_dual,
        past_dual_gap,
        past_velocity,
        past_velocity_gap,
    )


def solution(mesh):
    part = ("sector", "dom")
    in_specs = (
        P(None, part),
        P(None, part),
        P(part),
        P("sector", None),
        P(None, part),
        P(None, part),
        P(None, part),
        P(part),
        P(None, None, part),
        P(None, None, part),
        P(None, None, part),
        P(None, None, part),
    )
    out_specs = (P(None, part), P(None, part))
    return jax.shard_map(per_device, mesh=mesh, in_specs=in_specs, out_specs=out_specs, check_vma=False)
```

time: 753 us -> 94.8 us (0.13)
  waiting for transfers between devices: 368 us -> 0 us
  blocking collectives: 237 us -> 0 us
  Pallas kernels: 0 us -> 87.5 us
  other arithmetic: 69.6 us -> 0 us
  local copies, waits for them, and re-layouts: 43.1 us -> 5.33 us
  starting transfers between devices: 17.4 us -> 0 us
  between operations: 15.7 us -> 1.31 us
    psum x2 -> x0, waiting for transfers between devices: 363 us -> none  [per_device(): forces = lax.psum(own_forces, 'dom')]
    all_gather x3 -> x0, blocking collectives: 132 us -> none  [the longest x1 52.7 us: per_device(): lax.all_gather(velocity, 'dom', axis=1, tiled=True)]
    psum x1 -> x0, blocking collectives: 105 us -> none  [per_device(): gram, rhs = lax.psum((gram_local, rhs_local), ('sector', 'dom'))]
    pallas_call x0 -> x1, Pallas kernels: none -> 87.5 us  [per_device(): pl.pallas_call(functools.partial(kernel, sectors, doms), out_shape=(out,...]
    scatter-add x4 -> x0, other arithmetic: 46.1 us -> none  [the longest x2 28.9 us: per_device(): own_forces = partial_value[:, :sector_nodes].at[:, seam_list].add(seam_back)]
    gather x6 -> x0, local copies, waits for them, and re-layouts: 26.5 us -> none  [the longest x4 15.9 us: per_device(): seam_recv = seam_pull(sector_speed[:, seam_list])]
    ppermute x4 -> x0, starting transfers between devices: 17.4 us -> none  [shifted(): lax.ppermute(value, axis, [(i, (i + by) % size) for i in range(size)])]
    slice x6 -> x0, local copies, waits for them, and re-layouts: 12 us -> none  [the longest x2 8.79 us: per_device(): own_forces = partial_value[:, :sector_nodes].at[:, seam_list].add(seam_back)]
  transfers between devices with their start and end apart: 6 -> 0, of which waited for: 6 -> 0; matrix products, arithmetic and copies ran while one was open for 1% -> 0% of each run, Pallas kernels for 0% -> 0%
where the time goes in v1:
time: 94.8 us; the launch traced here: 94.1 us
  Pallas kernels  87.5 us (92%)
  local copies, waits for them, and re-layouts  5.33 us (6%)
  between operations  1.31 us (1%)
    pallas_call x1, Pallas kernels, per_device(): pl.pallas_call(functools.partial(kernel, sectors, doms), out_shape=(out,...  87.5 us
    unnamed x14, local copies, waits for them, and re-layouts  5.33 us

profile of v1, /device:TPU:1, one launch (start us, length us, event | category | flops | bytes accessed | tf_op | source)
XLA Modules:
  0.0 94.1 jit_solution(5134519285095952417)
XLA Ops:
  1.3 0.0 copy-start
  1.3 1.4 %copy.14.past_dual = f32[8,3,256]{2,1,0:T(4,128)} copy(f32[8,3,256]{2,0,1:T(8,128)} %param.20) | data formatting | bytes 49152 | tf_op args[8]
  2.6 0.0 copy-done
  2.7 0.0 copy-start.1
  2.7 0.6 copy.15.past_dual_gap
  3.3 0.1 copy-done.1
  3.4 0.0 copy-start.2
  3.4 0.6 copy.16.past_velocity
  4.0 0.1 copy-done.2
  4.1 0.6 copy.17.past_velocity_gap
  4.8 87.5 %dome.1 = (f32[3,256]{1,0:T(4,128)}, f32[3,256]{1,0:T(4,128)}) custom-call(f32[36,256]{1,0:T(8,128)} %strain.1, s32[4,256]{1,0:T(4,128)} %corner.1, s32[1]{0:T(128)S(6)} %copy.20.counts, s32[1,2048]{1,0:T(1,128)} %seam.1, f32[3,256]{1,0:T(4,128)} %velocity.1, f32[3,256]{1,0:T(4,128)} %dual.1, f32[3,256]{1,0:T(4,128)} %load.1, f32[2,128]{1,0:T(2,128)} %bitcast.1, ...), custom_call_target="tpu_custom_call" | custom-call | tf_op jit(solution)/shard_map/dome/pallas_call | solution.py:417
  92.2 0.0 copy-start.3
  92.2 1.3 %copy.21 = f32[3,256]{1,0:T(4,128)} copy(f32[3,256]{1,0:T(4,128)} %get-tuple-element.4) | data formatting | bytes 6144
  93.5 0.0 copy-done.3
  93.5 0.6 copy.22
Async XLA Ops:
  1.3 1.4 %copy-start = (f32[8,3,256]{2,0,1:T(8,128)S(1)}, f32[8,3,256]{2,0,1:T(8,128)}, u32[]{:S(2)}) copy-start(f32[8,3,256]{2,0,1:T(8,128)} %param.21) | copy-start | bytes 73732
  2.7 0.7 copy-start.1
  3.4 0.7 copy-start.2
  92.2 1.3 %copy-start.3 = (f32[3,256]{1,0:T(4,128)S(1)}, f32[3,256]{1,0:T(4,128)}, u32[]{:S(2)}) copy-start(f32[3,256]{1,0:T(4,128)} %get-tuple-element.5) | copy-start | bytes 9220

commit v2 on v1

--- a/solution.py
+++ b/solution.py
@@ -66,6 +66,8 @@
     force_in,
     push_in,
     onehot,
+    lhs_far,
+    lhs_near,
     gram_out,
     gram_in,
     total_out,
@@ -153,19 +155,9 @@
         block = speed_in.at[it, :, six]
         copy(block, block, 8 * it + 0, prev_sec, dom).wait()
 
-    def send_force(it):
-        def body(k, c):
-            d = far_first(k)
-            copy(force.at[it, 2 + d, six], force_in.at[it, dom, six], 8 * it + 3, next_sec, d).start()
-            return c
-
-        copy(force.at[it, 0, six], push_in.at[it, 1, six], 8 * it + 4, sec, left).start()
-        copy(force.at[it, 1, six], push_in.at[it, 0, six], 8 * it + 5, sec, right).start()
-        lax.fori_loop(0, doms, body, 0)
-
     def wait_force(it):
-        copy(force.at[it, 0, six], push_in.at[it, 1, six], 8 * it + 4, sec, left).wait()
-        copy(force.at[it, 1, six], push_in.at[it, 0, six], 8 * it + 5, sec, right).wait()
+        copy(force.at[it, doms, six], push_in.at[it, 1, six], 8 * it + 4, sec, left).wait()
+        copy(force.at[it, doms + 1, six], push_in.at[it, 0, six], 8 * it + 5, sec, right).wait()
         block = force_in.at[it, :, six]
         copy(block, block, 8 * it + 3, next_sec, dom).wait()
 
@@ -223,11 +215,9 @@
         acc = look(speed.at[it], 2, acc, 1)
         acc = look(edge_in.at[it, 1], 3, acc, 0)
 
-        def body(b, acc):
+        for b in range(doms):
             acc = look(speed_in.at[it, b], 4 + 2 * b, acc, 0)
-            return tuple(look(speed_in.at[it, b], 5 + 2 * b, acc, 1))
-
-        acc = lax.fori_loop(0, doms, body, tuple(acc))
+            acc = look(speed_in.at[it, b], 5 + 2 * b, acc, 1)
         rate = []
         for c in range(3):
             part = strain_r[3 * c] * acc[0] + strain_r[3 * c + 1] * acc[1] + strain_r[3 * c + 2] * acc[2]
@@ -255,29 +245,51 @@
         wanted = jnp.concatenate(wanted, axis=1)
         split = [jnp.concatenate(p, axis=1) for p in split]
 
-        def body(q, c):
-            total = jnp.zeros((16, LANES), jnp.float32)
+        def fill(lhs, q, keys):
+            hits = [wanted == k for k in keys]
             for s in range(3):
-                pair = [jnp.where(wanted == 4 * q + 2 * i, split[s], 0.0) for i in range(2)]
-                left_side = jnp.concatenate(pair, axis=0).astype(jnp.bfloat16)
-                total = total + lax.dot_general(
-                    left_side,
-                    onehot[...],
-                    (((1,), (1,)), ((), ())),
-                    preferred_element_type=jnp.float32,
-                )
-            force[it, 2 * q] = total[0:8]
-            force[it, 2 * q + 1] = total[8:16]
+                pair = jnp.concatenate([jnp.where(hit, split[s], 0.0) for hit in hits], axis=0)
+                lhs[s, pl.ds(pl.multiple_of(16 * q, 16), 16), :] = pair.astype(jnp.bfloat16)
+
+        def product(lhs):
+            rows = lhs.shape[1]
+            out = lax.dot_general(
+                lhs[...].reshape(3 * rows, 8 * LANES),
+                onehot[...],
+                (((1,), (1,)), ((), ())),
+                preferred_element_type=jnp.float32,
+            ).reshape(3, rows // 8, 8, LANES)
+            return (out[2] + out[1]) + out[0]
+
+        def fill_far(q, c):
+            fill(lhs_far, q, [4 + 2 * far_first(2 * q + i) for i in range(2)])
             return c
 
-        lax.fori_loop(0, (doms + 2) // 2, body, 0)
+        def fill_near(q, c):
+            fill(lhs_near, q, [4 + 2 * far_first(half + 2 * q + i) for i in range(2)])
+            return c
+
+        def send(k, c):
+            copy(force.at[it, k, six], force_in.at[it, dom, six], 8 * it + 3, next_sec, far_first(k)).start()
+            return c
+
+        half = doms // 2
+        lax.fori_loop(0, half // 2, fill_far, 0)
+        force[it, 0:half] = product(lhs_far)
+        lax.fori_loop(0, half, send, 0)
+        lax.fori_loop(0, half // 2, fill_near, 0)
+        fill(lhs_near, half // 2, [0, 2])
+        force[it, half : doms + 2] = product(lhs_near)
+        lax.fori_loop(half, doms, send, 0)
+        copy(force.at[it, doms, six], push_in.at[it, 1, six], 8 * it + 4, sec, left).start()
+        copy(force.at[it, doms + 1, six], push_in.at[it, 0, six], 8 * it + 5, sec, right).start()
 
     def next_speed(it):
         even = lax.rem(iota_row, 2) == 0
         own = jnp.where(
             even,
-            pltpu.roll(force[it, 0] + jnp.where(iota_row < 6, push_in[it, 0], 0.0), 7, 0),
-            pltpu.roll(force[it, 1] + jnp.where(iota_row < 6, push_in[it, 1], 0.0), 1, 0),
+            pltpu.roll(force[it, doms] + jnp.where(iota_row < 6, push_in[it, 0], 0.0), 7, 0),
+            pltpu.roll(force[it, doms + 1] + jnp.where(iota_row < 6, push_in[it, 1], 0.0), 1, 0),
         )
 
         def body(b, acc):
@@ -290,17 +302,15 @@
     wait_speed(0)
     dual_one, push = elements(0, dual_prev)
     spread(0, push)
-    send_force(0)
     wait_force(0)
     speed[1] = next_speed(0)
     send_speed(1)
     wait_speed(1)
     dual_two, push = elements(1, dual_one)
     spread(1, push)
-    send_force(1)
 
     def by_history(ref, j, h):
-        return ref[:, j, pl.ds(LANES * h, LANES)]
+        return ref[j, :, pl.ds(LANES * h, LANES)]
 
     depth = 8
     acc = [jnp.zeros((8, LANES), jnp.float32)] * (depth + 1)
@@ -431,6 +441,8 @@
             pltpu.VMEM((2, doms, 8, LANES), f32),
             pltpu.VMEM((2, 2, 8, LANES), f32),
             pltpu.VMEM((LANES, 8 * LANES), jnp.bfloat16),
+            pltpu.VMEM((3, 4 * doms, 8 * LANES), jnp.bfloat16),
+            pltpu.VMEM((3, 4 * doms + 16, 8 * LANES), jnp.bfloat16),
             pltpu.VMEM((1, 1, LANES), f32),
             pltpu.VMEM((doms, 1, LANES), f32),
             pltpu.VMEM((1, 1, LANES), f32),
@@ -449,10 +461,10 @@
         dual_state,
         nodal_load,
         mobility.reshape(2, LANES),
-        past_dual,
-        past_dual_gap,
-        past_velocity,
-        past_velocity_gap,
+        past_dual.transpose(1, 0, 2),
+        past_dual_gap.transpose(1, 0, 2),
+        past_velocity.transpose(1, 0, 2),
+        past_velocity_gap.transpose(1, 0, 2),
     )
 
 

time: 94.8 us -> 77.3 us (0.82)
  Pallas kernels: 87.5 us -> 73.7 us
  local copies, waits for them, and re-layouts: 5.33 us -> 1.86 us
    pallas_call x1, Pallas kernels: 87.5 us -> 73.7 us  [per_device(): pl.pallas_call(functools.partial(kernel, sectors, doms), out_shape=(out,...]
    unnamed x14 -> x4, local copies, waits for them, and re-layouts: 5.33 us -> 1.86 us
where the time goes in v2:
time: 77.3 us; the launch traced here: 76.8 us
  Pallas kernels  73.7 us (95%)
  local copies, waits for them, and re-layouts  1.86 us (2%)
  between operations  1.3 us (2%)
    pallas_call x1, Pallas kernels, per_device(): pl.pallas_call(functools.partial(kernel, sectors, doms), out_shape=(out,...  73.7 us
    unnamed x4, local copies, waits for them, and re-layouts  1.86 us

profile of v2, /device:TPU:1, one launch (start us, length us, event | category | flops | bytes accessed | tf_op | source)
XLA Modules:
  0.0 76.8 jit_solution(3836158661247014981)
XLA Ops:
  1.3 73.7 %dome.1 = (f32[3,256]{1,0:T(4,128)}, f32[3,256]{1,0:T(4,128)}) custom-call(f32[36,256]{1,0:T(8,128)} %strain.1, s32[4,256]{1,0:T(4,128)} %corner.1, s32[1]{0:T(128)S(6)} %copy.16.counts, s32[1,2048]{1,0:T(1,128)} %seam.1, f32[3,256]{1,0:T(4,128)} %velocity.1, f32[3,256]{1,0:T(4,128)} %dual.1, f32[3,256]{1,0:T(4,128)} %load.1, f32[2,128]{1,0:T(2,128)} %bitcast.9, ...), custom_call_target="tpu_custom_call" | custom-call | tf_op jit(solution)/shard_map/dome/pallas_call | solution.py:427
  75.0 0.0 copy-start
  75.0 1.3 %copy.17 = f32[3,256]{1,0:T(4,128)} copy(f32[3,256]{1,0:T(4,128)} %get-tuple-element.4) | data formatting | bytes 6144
  76.2 0.0 copy-done
  76.2 0.6 copy.18
Async XLA Ops:
  75.0 1.3 %copy-start = (f32[3,256]{1,0:T(4,128)S(1)}, f32[3,256]{1,0:T(4,128)}, u32[]{:S(2)}) copy-start(f32[3,256]{1,0:T(4,128)} %get-tuple-element.5) | copy-start | bytes 9220

commit v3 on v2

--- a/solution.py
+++ b/solution.py
@@ -41,10 +41,21 @@
 def kernel(
     sectors,
     doms,
+    strain_hbm,
+    corner_hbm,
+    counts,
+    seam_hbm,
+    velocity_hbm,
+    dual_hbm,
+    load_hbm,
+    mobility_hbm,
+    past_dual_hbm,
+    past_dual_gap_hbm,
+    past_velocity_hbm,
+    past_velocity_gap_hbm,
+    result,
     strain,
     corner,
-    counts,
-    seam,
     velocity,
     dual,
     load,
@@ -53,8 +64,6 @@
     past_dual_gap,
     past_velocity,
     past_velocity_gap,
-    new_velocity,
-    new_dual,
     speed,
     load6,
     mob6,
@@ -72,6 +81,9 @@
     gram_in,
     total_out,
     total_in,
+    mask_far,
+    mask_near,
+    load_sem,
     send_sem,
     recv_sem,
 ):
@@ -115,7 +127,27 @@
         signal(lax.rem(sec + o, sectors), dom)
         return c
 
+    loads = [
+        pltpu.make_async_copy(src, dst, load_sem.at[i])
+        for i, (src, dst) in enumerate(
+            [
+                (velocity_hbm, velocity),
+                (load_hbm, load),
+                (mobility_hbm, mobility),
+                (corner_hbm, corner),
+                (strain_hbm, strain),
+                (dual_hbm, dual),
+                (past_dual_gap_hbm, past_dual_gap),
+                (past_velocity_gap_hbm, past_velocity_gap),
+                (past_dual_hbm, past_dual),
+                (past_velocity_hbm, past_velocity),
+            ]
+        )
+    ]
+    loads[0].start()
     lax.fori_loop(0, doms, greet_dom, 0)
+    for l in loads[1:]:
+        l.start()
     lax.fori_loop(0, doms - 1, greet_own, 0)
     lax.fori_loop(2, sectors - 1, greet_sec, 0)
 
@@ -124,6 +156,8 @@
 
     speed[...] = jnp.zeros_like(speed)
     load6[...] = jnp.zeros_like(load6)
+    for l in loads[0:3]:
+        l.wait()
     for j in range(3):
         for h in range(2):
             r, cols = 2 * j + h, pl.ds(LANES * h, LANES)
@@ -149,22 +183,24 @@
         copy(speed.at[it, six], edge_in.at[it, 1, six], 8 * it + 2, sec, left).start()
         lax.fori_loop(0, doms, body, 0)
 
-    def wait_speed(it):
-        copy(speed.at[it, six], edge_in.at[it, 0, six], 8 * it + 1, sec, right).wait()
-        copy(speed.at[it, six], edge_in.at[it, 1, six], 8 * it + 2, sec, left).wait()
+    def wait_speed(it, what="wait_recv"):
+        getattr(copy(speed.at[it, six], edge_in.at[it, 0, six], 8 * it + 1, sec, right), what)()
+        getattr(copy(speed.at[it, six], edge_in.at[it, 1, six], 8 * it + 2, sec, left), what)()
         block = speed_in.at[it, :, six]
-        copy(block, block, 8 * it + 0, prev_sec, dom).wait()
-
-    def wait_force(it):
-        copy(force.at[it, doms, six], push_in.at[it, 1, six], 8 * it + 4, sec, left).wait()
-        copy(force.at[it, doms + 1, six], push_in.at[it, 0, six], 8 * it + 5, sec, right).wait()
+        getattr(copy(block, block, 8 * it + 0, prev_sec, dom), what)()
+
+    def wait_force(it, what="wait_recv"):
+        getattr(copy(force.at[it, doms, six], push_in.at[it, 1, six], 8 * it + 4, sec, left), what)()
+        getattr(copy(force.at[it, doms + 1, six], push_in.at[it, 0, six], 8 * it + 5, sec, right), what)()
         block = force_in.at[it, :, six]
-        copy(block, block, 8 * it + 3, next_sec, dom).wait()
-
-    seam_copy = copy(seam, seam_in, 6, prev_sec, dom)
+        getattr(copy(block, block, 8 * it + 3, next_sec, dom), what)()
+
+    seam_copy = copy(seam_hbm, seam_in, 6, prev_sec, dom)
     seam_copy.start()
     send_speed(0)
 
+    for l in loads[3:]:
+        l.wait()
     for c in range(3):
         for j in range(3):
             for k in range(4):
@@ -184,12 +220,12 @@
     ]
 
     sector_nodes = doms * 2 * LANES
-    seam_copy.wait()
+    seam_copy.wait_recv()
     position = nodes - sector_nodes
     place = jnp.bitwise_and(position, LANES - 1)
     place_row = jnp.right_shift(position, 7)
     seam_node = jnp.zeros((8, LANES), jnp.int32)
-    for r in range(seam.shape[1] // LANES):
+    for r in range(seam_in.shape[1] // LANES):
         row = jnp.broadcast_to(seam_in[0:1, LANES * r : LANES * (r + 1)], (8, LANES))
         seam_node = jnp.where(place_row == r, lane_take(row, place), seam_node)
     is_seam = position >= 0
@@ -200,6 +236,25 @@
     for t in range(8):
         hit = lane_is == jnp.broadcast_to(low[t : t + 1, :], (LANES, LANES))
         onehot[:, LANES * t : LANES * (t + 1)] = jnp.where(hit, 1.0, 0.0).astype(jnp.bfloat16)
+
+    half = doms // 2
+    wanted = jnp.concatenate([row_bcast(key, t) - jnp.bitwise_and(iota_row, 1) for t in range(8)], axis=1)
+
+    def mark(mask, q, keys):
+        pair = jnp.concatenate([jnp.where(wanted == k, 1.0, 0.0) for k in keys], axis=0)
+        mask[pl.ds(pl.multiple_of(16 * q, 16), 16), :] = pair.astype(jnp.bfloat16)
+
+    def mark_far(q, c):
+        mark(mask_far, q, [4 + 2 * far_first(2 * q + i) for i in range(2)])
+        return c
+
+    def mark_near(q, c):
+        mark(mask_near, q, [4 + 2 * far_first(half + 2 * q + i) for i in range(2)])
+        return c
+
+    lax.fori_loop(0, half // 2, mark_far, 0)
+    lax.fori_loop(0, half // 2, mark_near, 0)
+    mark(mask_near, half // 2, [0, 2])
 
     def elements(it, dual_now):
         def look(table, row_key, acc, h):
@@ -232,24 +287,24 @@
         return dual_next, push
 
     def spread(it, push):
-        wanted, split = [], [[], [], []]
+        split = [[], [], []]
         for t in range(8):
             value = jnp.where(iota_row < 2, row_bcast(push[0], t), row_bcast(push[1], t))
             value = jnp.where(iota_row < 4, value, row_bcast(push[2], t))
             value = jnp.where(iota_row < 6, value, 0.0)
-            wanted.append(row_bcast(key, t) - jnp.bitwise_and(iota_row, 1))
             for s in range(3):
                 piece = value.astype(jnp.bfloat16).astype(jnp.float32)
                 split[s].append(piece)
                 value = value - piece
-        wanted = jnp.concatenate(wanted, axis=1)
         split = [jnp.concatenate(p, axis=1) for p in split]
-
-        def fill(lhs, q, keys):
-            hits = [wanted == k for k in keys]
-            for s in range(3):
-                pair = jnp.concatenate([jnp.where(hit, split[s], 0.0) for hit in hits], axis=0)
-                lhs[s, pl.ds(pl.multiple_of(16 * q, 16), 16), :] = pair.astype(jnp.bfloat16)
+        split = [jnp.concatenate([p, p], axis=0).astype(jnp.bfloat16) for p in split]
+
+        def fill(lhs, mask):
+            for q in range(mask.shape[0] // 16):
+                rows = slice(16 * q, 16 * q + 16)
+                hit = mask[rows, :]
+                for s in range(3):
+                    lhs[s, rows, :] = hit * split[s]
 
         def product(lhs):
             rows = lhs.shape[1]
@@ -261,24 +316,14 @@
             ).reshape(3, rows // 8, 8, LANES)
             return (out[2] + out[1]) + out[0]
 
-        def fill_far(q, c):
-            fill(lhs_far, q, [4 + 2 * far_first(2 * q + i) for i in range(2)])
-            return c
-
-        def fill_near(q, c):
-            fill(lhs_near, q, [4 + 2 * far_first(half + 2 * q + i) for i in range(2)])
-            return c
-
         def send(k, c):
             copy(force.at[it, k, six], force_in.at[it, dom, six], 8 * it + 3, next_sec, far_first(k)).start()
             return c
 
-        half = doms // 2
-        lax.fori_loop(0, half // 2, fill_far, 0)
+        fill(lhs_far, mask_far)
         force[it, 0:half] = product(lhs_far)
         lax.fori_loop(0, half, send, 0)
-        lax.fori_loop(0, half // 2, fill_near, 0)
-        fill(lhs_near, half // 2, [0, 2])
+        fill(lhs_near, mask_near)
         force[it, half : doms + 2] = product(lhs_near)
         lax.fori_loop(half, doms, send, 0)
         copy(force.at[it, doms, six], push_in.at[it, 1, six], 8 * it + 4, sec, left).start()
@@ -352,7 +397,8 @@
 
     lax.fori_loop(0, doms - 1, send_gram, 0)
     block = gram_in.at[pl.ds(0, doms - 1)]
-    copy(block, block, 7, sec, dom).wait()
+    gram_copies = copy(block, block, 7, sec, dom)
+    gram_copies.wait_recv()
 
     def add_in(o, acc):
         return acc + gram_in[o]
@@ -366,43 +412,68 @@
 
     lax.fori_loop(1, sectors, send_total, 0)
     block = total_in.at[pl.ds(1, sectors - 1)]
-    copy(block, block, 14, sec, dom).wait()
+    total_copies = copy(block, block, 14, sec, dom)
+
+    def apart(now_row, past, past_gap):
+        return jnp.broadcast_to(now_row, (8, LANES)) - past - past_gap
+
+    parts = [(j, h) for j in range(3) for h in range(2)]
+    apart_u = [
+        apart(speed_two[2 * j + h : 2 * j + h + 1, :], by_history(past_velocity, j, h), by_history(past_velocity_gap, j, h))
+        for j, h in parts
+    ]
+    apart_w = [
+        apart(dual_two[j][4 * h : 4 * h + 1, :], by_history(past_dual, j, h), by_history(past_dual_gap, j, h))
+        for j, h in parts
+    ]
+    seam_copy.wait_send()
+    for it in range(ITERS):
+        wait_speed(it, "wait_send")
+        wait_force(it, "wait_send")
+    gram_copies.wait_send()
+    total_copies.wait_recv()
 
     def add_total(o, acc):
         return acc + total_in[o]
 
     total = lax.fori_loop(1, sectors, add_total, total)
 
-    system = jnp.zeros((8, LANES), jnp.float32)
-    for l in range(8):
-        row = total if l == 0 else pltpu.roll(total, LANES - 16 * l, 1)
-        system = jnp.where(iota_row == l, jnp.broadcast_to(row, (8, LANES)), system)
-
-    diagonal = iota_row == iota_lane
-    trace = jnp.sum(jnp.where(diagonal, system, 0.0), axis=1, keepdims=True)
-    trace = jnp.sum(trace, axis=0, keepdims=True)
-    ridge = jnp.broadcast_to(0.0001 * trace / depth, (8, LANES))
-    system = jnp.where(diagonal, system + ridge, system)
+    def entry(lane):
+        return jnp.broadcast_to(jnp.broadcast_to(total[:, lane : lane + 1], (1, LANES)), (8, LANES))
+
+    upper = [[entry(16 * i + l) if l >= i else None for l in range(depth + 1)] for i in range(depth)]
+    trace = upper[0][0]
+    for i in range(1, depth):
+        trace = trace + upper[i][i]
+    ridge = 0.0001 * trace / depth
+    for i in range(depth):
+        upper[i][i] = upper[i][i] + ridge
+    inverse = []
     for k in range(depth):
-        pivot_row = row_bcast(system, k)
-        pivot_row = pivot_row / jnp.broadcast_to(pivot_row[:, k : k + 1], (8, LANES))
-        column = jnp.broadcast_to(system[:, k : k + 1], (8, LANES))
-        system = jnp.where(iota_row == k, pivot_row, system - column * pivot_row)
-    coeffs = jnp.broadcast_to(system[:, depth : depth + 1], (8, LANES))
-
-    def mixed(now_row, past, past_gap):
-        now = jnp.broadcast_to(now_row, (8, LANES))
-        return now_row - jnp.sum(coeffs * (now - past - past_gap), axis=0, keepdims=True)
-
-    for j in range(3):
-        for h in range(2):
-            r, cols = 2 * j + h, pl.ds(LANES * h, LANES)
-            new_velocity[j : j + 1, cols] = mixed(
-                speed_two[r : r + 1, :], by_history(past_velocity, j, h), by_history(past_velocity_gap, j, h)
-            )
-            new_dual[j : j + 1, cols] = mixed(
-                dual_two[j][4 * h : 4 * h + 1, :], by_history(past_dual, j, h), by_history(past_dual_gap, j, h)
-            )
+        inverse.append(1.0 / upper[k][k])
+        for i in range(k + 1, depth):
+            scale = upper[k][i] * inverse[k]
+            for l in range(i, depth + 1):
+                upper[i][l] = upper[i][l] - scale * upper[k][l]
+    solved = [None] * depth
+    for k in reversed(range(depth)):
+        value = upper[k][depth]
+        for l in range(k + 1, depth):
+            value = value - upper[k][l] * solved[l]
+        solved[k] = value * inverse[k]
+    coeffs = solved[0]
+    for i in range(1, depth):
+        coeffs = jnp.where(iota_row == i, solved[i], coeffs)
+
+    for p, (j, h) in enumerate(parts):
+        cols = pl.ds(LANES * h, LANES)
+        result[j : j + 1, cols] = speed_two[2 * j + h : 2 * j + h + 1, :] - jnp.sum(
+            coeffs * apart_u[p], axis=0, keepdims=True
+        )
+        result[4 + j : 5 + j, cols] = dual_two[j][4 * h : 4 * h + 1, :] - jnp.sum(
+            coeffs * apart_w[p], axis=0, keepdims=True
+        )
+    total_copies.wait_send()
 
 
 def per_device(
@@ -423,13 +494,25 @@
     out = jax.ShapeDtypeStruct(velocity.shape, jnp.float32)
     vmem = pl.BlockSpec(memory_space=pltpu.VMEM)
     smem = pl.BlockSpec(memory_space=pltpu.SMEM)
+    hbm = pl.BlockSpec(memory_space=pl.ANY)
+    history = pltpu.VMEM((3, 8, 2 * LANES), jnp.float32)
     f32 = jnp.float32
-    return pl.pallas_call(
+    result = pl.pallas_call(
         functools.partial(kernel, sectors, doms),
-        out_shape=(out, out),
-        in_specs=[vmem, vmem, smem] + [vmem] * 9,
-        out_specs=(vmem, vmem),
+        out_shape=pltpu.VMEM((8, 2 * LANES), f32),
+        in_specs=[hbm, hbm, smem] + [hbm] * 9,
+        out_specs=vmem,
         scratch_shapes=[
+            pltpu.VMEM(strain_map.shape, f32),
+            pltpu.VMEM(corner_nodes.shape, jnp.int32),
+            pltpu.VMEM(velocity.shape, f32),
+            pltpu.VMEM(dual_state.shape, f32),
+            pltpu.VMEM(nodal_load.shape, f32),
+            pltpu.VMEM((2, LANES), f32),
+            history,
+            history,
+            history,
+            history,
             pltpu.VMEM((2, 8, LANES), f32),
             pltpu.VMEM((8, LANES), f32),
             pltpu.VMEM((8, LANES), f32),
@@ -447,6 +530,9 @@
             pltpu.VMEM((doms, 1, LANES), f32),
             pltpu.VMEM((1, 1, LANES), f32),
             pltpu.VMEM((sectors, 1, LANES), f32),
+            pltpu.VMEM((4 * doms, 8 * LANES), jnp.bfloat16),
+            pltpu.VMEM((4 * doms + 16, 8 * LANES), jnp.bfloat16),
+            pltpu.SemaphoreType.DMA((10,)),
             pltpu.SemaphoreType.DMA((16,)),
             pltpu.SemaphoreType.DMA((16,)),
         ],
@@ -466,6 +552,7 @@
         past_velocity.transpose(1, 0, 2),
         past_velocity_gap.transpose(1, 0, 2),
     )
+    return result[0:3], result[4:7]
 
 
 def solution(mesh):

time: 77.3 us -> 74.3 us (0.961)
  Pallas kernels: 73.7 us -> 71.8 us
  local copies, waits for them, and re-layouts: 1.86 us -> 0.6 us
    pallas_call x1, Pallas kernels: 73.7 us -> 71.8 us  [per_device(): pl.pallas_call(functools.partial(kernel, sectors, doms), out_shape=pltpu....]
    unnamed x4 -> x0, local copies, waits for them, and re-layouts: 1.86 us -> none
where the time goes in v3:
time: 74.3 us; the launch traced here: 73.7 us
  Pallas kernels  71.8 us (97%)
  between operations  1.29 us (2%)
    pallas_call x1, Pallas kernels, per_device(): pl.pallas_call(functools.partial(kernel, sectors, doms), out_shape=pltpu....  71.8 us

profile of v3, /device:TPU:1, one launch (start us, length us, event | category | flops | bytes accessed | tf_op | source)
XLA Modules:
  0.0 73.7 jit_solution(15407890752024155852)
XLA Ops:
  1.3 71.8 %dome.1 = f32[8,256]{1,0:T(8,128)S(1)} custom-call(f32[36,256]{1,0:T(8,128)} %strain_hbm.1, s32[4,256]{1,0:T(4,128)} %corner_hbm.1, s32[1]{0:T(128)S(6)} %copy.14.counts, s32[1,2048]{1,0:T(1,128)} %seam_hbm.1, f32[3,256]{1,0:T(4,128)} %velocity_hbm.1, f32[3,256]{1,0:T(4,128)} %dual_hbm.1, f32[3,256]{1,0:T(4,128)} %load_hbm.1, f32[2,128]{1,0:T(2,128)} %bitcast.9, ...), custom_call_target="tpu_custom_call" | custom-call | tf_op jit(solution)/shard_map/dome/pallas_call | solution.py:500
  73.1 0.6 fusion

commit v4 on v3

--- a/solution.py
+++ b/solution.py
@@ -113,14 +113,24 @@
     def signal(s, d):
         pl.semaphore_signal(barrier, inc=1, device_id=(s, d), device_id_type=MESH)
 
-    def greet_dom(k, c):
-        d = far_first(k)
-        signal(prev_sec, d)
-        signal(next_sec, d)
-        return c
-
-    def greet_own(k, c):
-        signal(sec, far_first(k))
+    chips = doms // 2
+    reach = chips // 4
+    back, ahead = reach, max(reach - 1, 1)
+    chip, core = dom // 2, lax.rem(dom, 2)
+
+    def at(offset, c):
+        return 2 * lax.rem(chip + offset + chips, chips) + c
+
+    def greet_next(k, c):
+        signal(next_sec, at(k // 2 - reach, lax.rem(k, 2)))
+        return c
+
+    def greet_back(k, c):
+        signal(sec, at(k // 2 - back, lax.rem(k, 2)))
+        return c
+
+    def greet_ahead(k, c):
+        signal(sec, at(k // 2 + 1, lax.rem(k, 2)))
         return c
 
     def greet_sec(o, c):
@@ -145,11 +155,13 @@
         )
     ]
     loads[0].start()
-    lax.fori_loop(0, doms, greet_dom, 0)
+    lax.fori_loop(0, 2 * (2 * reach + 1), greet_next, 0)
+    lax.fori_loop(0, 2 * back, greet_back, 0)
+    lax.fori_loop(0, 2 * ahead, greet_ahead, 0)
+    signal(sec, at(0, 1 - core))
+    lax.fori_loop(2, sectors - 1, greet_sec, 0)
     for l in loads[1:]:
         l.start()
-    lax.fori_loop(0, doms - 1, greet_own, 0)
-    lax.fori_loop(2, sectors - 1, greet_sec, 0)
 
     iota_row = lax.broadcasted_iota(jnp.int32, (8, LANES), 0)
     iota_lane = lax.broadcasted_iota(jnp.int32, (8, LANES), 1)
@@ -169,35 +181,86 @@
         jnp.broadcast_to(mobility[1:2, :], (8, LANES)),
     )
 
-    pl.semaphore_wait(barrier, 2 * doms + (doms - 1) + (sectors - 3))
+    pl.semaphore_wait(barrier, 2 * (2 * reach + 1) + 2 * (back + ahead) + 1 + (sectors - 3))
 
     six = pl.ds(0, 6)
 
-    def send_speed(it):
+    def send_edges(it):
+        copy(speed.at[it, six], edge_in.at[it, 0, six], 1 + 2 * it, sec, right).start()
+        copy(speed.at[it, six], edge_in.at[it, 1, six], 2 + 2 * it, sec, left).start()
+
+    def wait_edges(it, what):
+        getattr(copy(speed.at[it, six], edge_in.at[it, 0, six], 1 + 2 * it, sec, right), what)()
+        getattr(copy(speed.at[it, six], edge_in.at[it, 1, six], 2 + 2 * it, sec, left), what)()
+
+    def some_blocks(count, sem):
+        block = speed_in.at[0, pl.ds(0, count), six]
+        return copy(block, block, sem, prev_sec, dom)
+
+    def relay_copy(offset, sem):
+        return copy(speed.at[0, six], speed_in.at[0, dom, six], sem, prev_sec, at(offset, core))
+
+    def send_first():
+        def direct(offset, c):
+            copy(speed.at[0, six], speed_in.at[0, dom, six], 0, prev_sec, at(offset, c)).start()
+
+        relay_copy(reach, 6).start()
+        relay_copy(-reach, 7).start()
+        direct(reach, 1 - core)
+        direct(-reach, 1 - core)
+        for offset in range(reach - 1, -1, -1):
+            for o in sorted({offset, -offset}):
+                for c in range(2):
+                    direct(o, c)
+        send_edges(0)
+
+    def pass_on():
+        def forward(src, sem, offset, c):
+            copy(speed_in.at[0, src, six], speed_in.at[0, src, six], sem, sec, at(offset, c)).start()
+
+        relay_copy(reach, 6).wait_recv()
+        for m in range(reach, 0, -1):
+            for c in range(2):
+                forward(at(-reach, core), 8, m, c)
+        relay_copy(-reach, 7).wait_recv()
+        for m in range(reach - 1, 0, -1):
+            for c in range(2):
+                forward(at(reach, core), 8, -m, c)
+
+    def wait_first():
+        wait_edges(0, "wait_recv")
+        some_blocks(4 * reach, 0).wait_recv()
+        some_blocks(2 * (2 * reach - 1), 8).wait_recv()
+
+    def wait_first_sends():
+        wait_edges(0, "wait_send")
+        relay_copy(reach, 6).wait_send()
+        relay_copy(-reach, 7).wait_send()
+        some_blocks(4 * reach, 0).wait_send()
+        some_blocks(2 * (2 * reach - 1), 8).wait_send()
+
+    def send_second():
         def body(k, c):
-            d = far_first(k)
-            copy(speed.at[it, six], speed_in.at[it, dom, six], 8 * it + 0, prev_sec, d).start()
+            copy(speed.at[1, six], speed_in.at[1, dom, six], 9, prev_sec, far_first(k)).start()
             return c
 
-        copy(speed.at[it, six], edge_in.at[it, 0, six], 8 * it + 1, sec, right).start()
-        copy(speed.at[it, six], edge_in.at[it, 1, six], 8 * it + 2, sec, left).start()
         lax.fori_loop(0, doms, body, 0)
-
-    def wait_speed(it, what="wait_recv"):
-        getattr(copy(speed.at[it, six], edge_in.at[it, 0, six], 8 * it + 1, sec, right), what)()
-        getattr(copy(speed.at[it, six], edge_in.at[it, 1, six], 8 * it + 2, sec, left), what)()
-        block = speed_in.at[it, :, six]
-        getattr(copy(block, block, 8 * it + 0, prev_sec, dom), what)()
+        send_edges(1)
+
+    def wait_second(what):
+        wait_edges(1, what)
+        block = speed_in.at[1, :, six]
+        getattr(copy(block, block, 9, prev_sec, dom), what)()
 
     def wait_force(it, what="wait_recv"):
-        getattr(copy(force.at[it, doms, six], push_in.at[it, 1, six], 8 * it + 4, sec, left), what)()
-        getattr(copy(force.at[it, doms + 1, six], push_in.at[it, 0, six], 8 * it + 5, sec, right), what)()
+        getattr(copy(force.at[it, doms, six], push_in.at[it, 1, six], 12 + 2 * it, sec, left), what)()
+        getattr(copy(force.at[it, doms + 1, six], push_in.at[it, 0, six], 13 + 2 * it, sec, right), what)()
         block = force_in.at[it, :, six]
-        getattr(copy(block, block, 8 * it + 3, next_sec, dom), what)()
-
-    seam_copy = copy(seam_hbm, seam_in, 6, prev_sec, dom)
+        getattr(copy(block, block, 10 + it, next_sec, dom), what)()
+
+    seam_copy = copy(seam_hbm, seam_in, 5, prev_sec, dom)
+    send_first()
     seam_copy.start()
-    send_speed(0)
 
     for l in loads[3:]:
         l.wait()
@@ -219,6 +282,8 @@
         for c in range(3)
     ]
 
+    pass_on()
+
     sector_nodes = doms * 2 * LANES
     seam_copy.wait_recv()
     position = nodes - sector_nodes
@@ -317,7 +382,7 @@
             return (out[2] + out[1]) + out[0]
 
         def send(k, c):
-            copy(force.at[it, k, six], force_in.at[it, dom, six], 8 * it + 3, next_sec, far_first(k)).start()
+            copy(force.at[it, k, six], force_in.at[it, dom, six], 10 + it, next_sec, far_first(k)).start()
             return c
 
         fill(lhs_far, mask_far)
@@ -326,8 +391,8 @@
         fill(lhs_near, mask_near)
         force[it, half : doms + 2] = product(lhs_near)
         lax.fori_loop(half, doms, send, 0)
-        copy(force.at[it, doms, six], push_in.at[it, 1, six], 8 * it + 4, sec, left).start()
-        copy(force.at[it, doms + 1, six], push_in.at[it, 0, six], 8 * it + 5, sec, right).start()
+        copy(force.at[it, doms, six], push_in.at[it, 1, six], 12 + 2 * it, sec, left).start()
+        copy(force.at[it, doms + 1, six], push_in.at[it, 0, six], 13 + 2 * it, sec, right).start()
 
     def next_speed(it):
         even = lax.rem(iota_row, 2) == 0
@@ -344,13 +409,13 @@
         step = speed[it] - mob6[...] * (own - load6[...])
         return jnp.where(iota_row < 6, step, 0.0)
 
-    wait_speed(0)
+    wait_first()
     dual_one, push = elements(0, dual_prev)
     spread(0, push)
     wait_force(0)
     speed[1] = next_speed(0)
-    send_speed(1)
-    wait_speed(1)
+    send_second()
+    wait_second("wait_recv")
     dual_two, push = elements(1, dual_one)
     spread(1, push)
 
@@ -392,12 +457,12 @@
     gram_out[0] = fold(packed)
 
     def send_gram(k, c):
-        copy(gram_out.at[0], gram_in.at[k], 7, sec, far_first(k)).start()
+        copy(gram_out.at[0], gram_in.at[k], 16, sec, far_first(k)).start()
         return c
 
     lax.fori_loop(0, doms - 1, send_gram, 0)
     block = gram_in.at[pl.ds(0, doms - 1)]
-    gram_copies = copy(block, block, 7, sec, dom)
+    gram_copies = copy(block, block, 16, sec, dom)
     gram_copies.wait_recv()
 
     def add_in(o, acc):
@@ -407,12 +472,12 @@
     total_out[0] = total
 
     def send_total(o, c):
-        copy(total_out.at[0], total_in.at[o], 14, lax.rem(sec + o, sectors), dom).start()
+        copy(total_out.at[0], total_in.at[o], 17, lax.rem(sec + o, sectors), dom).start()
         return c
 
     lax.fori_loop(1, sectors, send_total, 0)
     block = total_in.at[pl.ds(1, sectors - 1)]
-    total_copies = copy(block, block, 14, sec, dom)
+    total_copies = copy(block, block, 17, sec, dom)
 
     def apart(now_row, past, past_gap):
         return jnp.broadcast_to(now_row, (8, LANES)) - past - past_gap
@@ -427,8 +492,9 @@
         for j, h in parts
     ]
     seam_copy.wait_send()
+    wait_first_sends()
+    wait_second("wait_send")
     for it in range(ITERS):
-        wait_speed(it, "wait_send")
         wait_force(it, "wait_send")
     gram_copies.wait_send()
     total_copies.wait_recv()
@@ -533,8 +599,8 @@
             pltpu.VMEM((4 * doms, 8 * LANES), jnp.bfloat16),
             pltpu.VMEM((4 * doms + 16, 8 * LANES), jnp.bfloat16),
             pltpu.SemaphoreType.DMA((10,)),
-            pltpu.SemaphoreType.DMA((16,)),
-            pltpu.SemaphoreType.DMA((16,)),
+            pltpu.SemaphoreType.DMA((18,)),
+            pltpu.SemaphoreType.DMA((18,)),
         ],
         compiler_params=pltpu.CompilerParams(collective_id=0, has_side_effects=True),
         name="dome",

time: 74.3 us -> 72.4 us (0.974)
  Pallas kernels: 71.8 us -> 69.8 us
    pallas_call x1, Pallas kernels: 71.8 us -> 69.8 us  [per_device(): pl.pallas_call(functools.partial(kernel, sectors, doms), out_shape=pltpu....]
where the time goes in v4:
time: 72.4 us; the launch traced here: 71.7 us
  Pallas kernels  69.8 us (96%)
  between operations  1.29 us (2%)
    pallas_call x1, Pallas kernels, per_device(): pl.pallas_call(functools.partial(kernel, sectors, doms), out_shape=pltpu....  69.8 us

profile of v4, /device:TPU:1, one launch (start us, length us, event | category | flops | bytes accessed | tf_op | source)
XLA Modules:
  0.0 71.7 jit_solution(8655331956598416679)
XLA Ops:
  1.3 69.8 %dome.1 = f32[8,256]{1,0:T(8,128)S(1)} custom-call(f32[36,256]{1,0:T(8,128)} %strain_hbm.1, s32[4,256]{1,0:T(4,128)} %corner_hbm.1, s32[1]{0:T(128)S(6)} %copy.14.counts, s32[1,2048]{1,0:T(1,128)} %seam_hbm.1, f32[3,256]{1,0:T(4,128)} %velocity_hbm.1, f32[3,256]{1,0:T(4,128)} %dual_hbm.1, f32[3,256]{1,0:T(4,128)} %load_hbm.1, f32[2,128]{1,0:T(2,128)} %bitcast.9, ...), custom_call_target="tpu_custom_call" | custom-call | tf_op jit(solution)/shard_map/dome/pallas_call | solution.py:566
  71.1 0.6 fusion

commit v5 on v4

--- a/solution.py
+++ b/solution.py
@@ -43,7 +43,7 @@
     doms,
     strain_hbm,
     corner_hbm,
-    counts,
+    counts_hbm,
     seam_hbm,
     velocity_hbm,
     dual_hbm,
@@ -54,6 +54,7 @@
     past_velocity_hbm,
     past_velocity_gap_hbm,
     result,
+    counts,
     strain,
     corner,
     velocity,
@@ -68,7 +69,15 @@
     load6,
     mob6,
     strain_r,
+    own_seam,
     seam_in,
+    base_out,
+    base_in,
+    own_out,
+    own_in,
+    seam_out,
+    seam_part,
+    seam_speed,
     speed_in,
     edge_in,
     force,
@@ -84,6 +93,7 @@
     mask_far,
     mask_near,
     load_sem,
+    ready,
     send_sem,
     recv_sem,
 ):
@@ -115,7 +125,7 @@
 
     chips = doms // 2
     reach = chips // 4
-    back, ahead = reach, max(reach - 1, 1)
+    back, ahead = reach, reach
     chip, core = dom // 2, lax.rem(dom, 2)
 
     def at(offset, c):
@@ -151,6 +161,8 @@
                 (past_velocity_gap_hbm, past_velocity_gap),
                 (past_dual_hbm, past_dual),
                 (past_velocity_hbm, past_velocity),
+                (counts_hbm, counts),
+                (seam_hbm, own_seam),
             ]
         )
     ]
@@ -218,11 +230,16 @@
         def forward(src, sem, offset, c):
             copy(speed_in.at[0, src, six], speed_in.at[0, src, six], sem, sec, at(offset, c)).start()
 
+        def answer(offset):
+            pl.semaphore_signal(ready, inc=1, device_id=(next_sec, at(offset, core)), device_id_type=MESH)
+
         relay_copy(reach, 6).wait_recv()
+        answer(-reach)
         for m in range(reach, 0, -1):
             for c in range(2):
                 forward(at(-reach, core), 8, m, c)
         relay_copy(-reach, 7).wait_recv()
+        answer(reach)
         for m in range(reach - 1, 0, -1):
             for c in range(2):
                 forward(at(reach, core), 8, -m, c)
@@ -239,24 +256,41 @@
         some_blocks(4 * reach, 0).wait_send()
         some_blocks(2 * (2 * reach - 1), 8).wait_send()
 
-    def send_second():
-        def body(k, c):
-            copy(speed.at[1, six], speed_in.at[1, dom, six], 9, prev_sec, far_first(k)).start()
-            return c
-
-        lax.fori_loop(0, doms, body, 0)
-        send_edges(1)
-
-    def wait_second(what):
-        wait_edges(1, what)
-        block = speed_in.at[1, :, six]
-        getattr(copy(block, block, 9, prev_sec, dom), what)()
+    def all_small(ref, count, sem):
+        block = ref.at[pl.ds(0, count)]
+        return copy(block, block, sem, sec, dom)
+
+    def small_wait(i, what):
+        ref, count, sem = [(base_in, doms, 18), (own_in, doms, 19), (seam_part, doms - 1, 20), (seam_speed, doms - 1, 9)][i]
+        getattr(all_small(ref, count, sem), what)()
+
+    def send_base(k, c):
+        d = far_first(k)
+        copy(base_out.at[d], base_in.at[dom], 18, prev_sec, d).start()
+        return c
+
+    def send_own(k, c):
+        d = far_first(k)
+        copy(own_out.at[d], own_in.at[dom], 19, prev_sec, d).start()
+        return c
+
+    def send_seam(k, c):
+        d = far_first(k)
+        copy(seam_out.at[d], seam_part.at[dom], 20, sec, d).start()
+        return c
+
+    def send_seam_speed(k, c):
+        copy(seam_speed.at[dom], seam_speed.at[dom], 9, sec, far_first(k)).start()
+        return c
 
     def wait_force(it, what="wait_recv"):
         getattr(copy(force.at[it, doms, six], push_in.at[it, 1, six], 12 + 2 * it, sec, left), what)()
         getattr(copy(force.at[it, doms + 1, six], push_in.at[it, 0, six], 13 + 2 * it, sec, right), what)()
         block = force_in.at[it, :, six]
         getattr(copy(block, block, 10 + it, next_sec, dom), what)()
+
+    for offset in (reach, -reach):
+        pl.semaphore_signal(ready, inc=1, device_id=(sec, at(offset, core)), device_id_type=MESH)
 
     seam_copy = copy(seam_hbm, seam_in, 5, prev_sec, dom)
     send_first()
@@ -321,6 +355,82 @@
     lax.fori_loop(0, half // 2, mark_near, 0)
     mark(mask_near, half // 2, [0, 2])
 
+    low_half = iota_lane < LANES // 2
+    groups = own_seam.shape[1] // (8 * LANES)
+
+    def positions(ref, g):
+        rows = [ref[0:1, LANES * (8 * g + r) : LANES * (8 * g + r + 1)] for r in range(8)]
+        node = jnp.concatenate(rows, axis=0)
+        return jnp.right_shift(node, 7), jnp.bitwise_and(node, LANES - 1)
+
+    def swap(x):
+        return pltpu.roll(x, LANES // 2, 1)
+
+    def write_messages(ref, g, first, second, third, fourth):
+        even = (jnp.where(low_half, first, swap(second)), jnp.where(low_half, third, swap(fourth)))
+        odd = (jnp.where(low_half, swap(first), second), jnp.where(low_half, swap(third), fourth))
+        for r in range(8):
+            for parity, rows in enumerate((even, odd)):
+                for i in range(2):
+                    ref[2 * (8 * g + r) + parity, i : i + 1, :] = rows[i][r : r + 1, :]
+
+    zero = jnp.zeros((8, LANES), jnp.float32)
+    base6 = speed[0] + mob6[...] * load6[...]
+    for g in range(groups):
+        node_row, node_lane = positions(own_seam, g)
+        found = [zero] * 4
+        for h in range(2):
+            hit = node_row == 2 * dom + h
+            for j in range(4):
+                row = row_bcast(base6, 2 * j + h) if j < 3 else row_bcast(mob6[...], h)
+                found[j] = jnp.where(hit, lane_take(row, node_lane), found[j])
+        write_messages(base_out, g, *found)
+
+    def seam_forces():
+        for g in range(groups):
+            node_row, node_lane = positions(seam_in, g)
+            found = [zero] * 3
+            for k in range(doms):
+                block = force[0, k]
+                for h in range(2):
+                    hit = node_row == 2 * far_first(k) + h
+                    for j in range(3):
+                        found[j] = jnp.where(hit, lane_take(row_bcast(block, 2 * j + h), node_lane), found[j])
+            write_messages(seam_out, g, *found, zero)
+
+    def own_forces():
+        for g in range(groups):
+            node_row, node_lane = positions(own_seam, g)
+            found = [zero] * 3
+            for row_key in range(4):
+                block = force[0, doms + row_key // 2]
+                hit = node_row - 2 * dom + 1 == row_key
+                for j in range(3):
+                    row = row_bcast(block, 2 * j + row_key % 2)
+                    found[j] = jnp.where(hit, lane_take(row, node_lane), found[j])
+            write_messages(own_out, g, *found, zero)
+
+    def sum_blocks(refs):
+        group = [ref[b] for ref in refs for b in range(doms)]
+        while len(group) > 1:
+            group = [x + y for x, y in zip(group[::2], group[1::2])] + group[len(group) - len(group) % 2 :]
+        return group[0]
+
+    def collect():
+        seam_part[dom] = seam_out[dom]
+        small_wait(0, "wait_recv")
+        base = sum_blocks([base_in])
+        half_lane = lax.broadcasted_iota(jnp.int32, (2, LANES), 1) < LANES // 2
+        last = jnp.broadcast_to(base[1:2, :], (2, LANES))
+        step = jnp.where(half_lane, pltpu.roll(last, LANES // 2, 1), last)
+        small_wait(1, "wait_recv")
+        small_wait(2, "wait_recv")
+        seam_speed[dom] = base - step * sum_blocks([own_in, seam_part])
+        lax.fori_loop(0, doms - 1, send_seam_speed, 0)
+
+    collector = jnp.where(is_seam, jnp.right_shift(position, 6), -1)
+    place_low = jnp.bitwise_and(position, LANES // 2 - 1)
+
     def elements(it, dual_now):
         def look(table, row_key, acc, h):
             out = []
@@ -336,8 +446,14 @@
         acc = look(edge_in.at[it, 1], 3, acc, 0)
 
         for b in range(doms):
-            acc = look(speed_in.at[it, b], 4 + 2 * b, acc, 0)
-            acc = look(speed_in.at[it, b], 5 + 2 * b, acc, 1)
+            if it == 0:
+                acc = look(speed_in.at[it, b], 4 + 2 * b, acc, 0)
+                acc = look(speed_in.at[it, b], 5 + 2 * b, acc, 1)
+            else:
+                hit = collector == b
+                rows = [jnp.broadcast_to(seam_speed[b, i : i + 1, :], (8, LANES)) for i in range(2)]
+                picks = [(rows[0], place_low), (rows[0], place_low + LANES // 2), (rows[1], place_low)]
+                acc = [jnp.where(hit, lane_take(*pick), x) for pick, x in zip(picks, acc)]
         rate = []
         for c in range(3):
             part = strain_r[3 * c] * acc[0] + strain_r[3 * c + 1] * acc[1] + strain_r[3 * c + 2] * acc[2]
@@ -387,9 +503,16 @@
 
         fill(lhs_far, mask_far)
         force[it, 0:half] = product(lhs_far)
-        lax.fori_loop(0, half, send, 0)
+        if it == 1:
+            lax.fori_loop(0, half, send, 0)
         fill(lhs_near, mask_near)
         force[it, half : doms + 2] = product(lhs_near)
+        if it == 0:
+            own_forces()
+            lax.fori_loop(0, doms, send_own, 0)
+            seam_forces()
+            lax.fori_loop(0, doms - 1, send_seam, 0)
+            lax.fori_loop(0, half, send, 0)
         lax.fori_loop(half, doms, send, 0)
         copy(force.at[it, doms, six], push_in.at[it, 1, six], 12 + 2 * it, sec, left).start()
         copy(force.at[it, doms + 1, six], push_in.at[it, 0, six], 13 + 2 * it, sec, right).start()
@@ -402,20 +525,25 @@
             pltpu.roll(force[it, doms + 1] + jnp.where(iota_row < 6, push_in[it, 1], 0.0), 1, 0),
         )
 
-        def body(b, acc):
-            return acc + force_in[it, b]
-
-        own = lax.fori_loop(0, doms, body, own)
+        for b in range(0, doms, 8):
+            group = [force_in[it, b + i] for i in range(8)]
+            while len(group) > 1:
+                group = [x + y for x, y in zip(group[::2], group[1::2])]
+            own = own + group[0]
         step = speed[it] - mob6[...] * (own - load6[...])
         return jnp.where(iota_row < 6, step, 0.0)
 
     wait_first()
+    pl.semaphore_wait(ready, 4)
+    lax.fori_loop(0, doms, send_base, 0)
     dual_one, push = elements(0, dual_prev)
     spread(0, push)
+    collect()
     wait_force(0)
     speed[1] = next_speed(0)
-    send_second()
-    wait_second("wait_recv")
+    send_edges(1)
+    wait_edges(1, "wait_recv")
+    small_wait(3, "wait_recv")
     dual_two, push = elements(1, dual_one)
     spread(1, push)
 
@@ -465,10 +593,13 @@
     gram_copies = copy(block, block, 16, sec, dom)
     gram_copies.wait_recv()
 
-    def add_in(o, acc):
-        return acc + gram_in[o]
-
-    total = lax.fori_loop(0, doms - 1, add_in, gram_out[0])
+    def add_all(own, ref, first, last):
+        group = [own] + [ref[o] for o in range(first, last)]
+        while len(group) > 1:
+            group = [x + y for x, y in zip(group[::2], group[1::2])] + group[len(group) - len(group) % 2 :]
+        return group[0]
+
+    total = add_all(gram_out[0], gram_in, 0, doms - 1)
     total_out[0] = total
 
     def send_total(o, c):
@@ -493,16 +624,15 @@
     ]
     seam_copy.wait_send()
     wait_first_sends()
-    wait_second("wait_send")
+    wait_edges(1, "wait_send")
+    for i in range(4):
+        small_wait(i, "wait_send")
     for it in range(ITERS):
         wait_force(it, "wait_send")
     gram_copies.wait_send()
     total_copies.wait_recv()
 
-    def add_total(o, acc):
-        return acc + total_in[o]
-
-    total = lax.fori_loop(1, sectors, add_total, total)
+    total = add_all(total, total_in, 1, sectors)
 
     def entry(lane):
         return jnp.broadcast_to(jnp.broadcast_to(total[:, lane : lane + 1], (1, LANES)), (8, LANES))
@@ -559,16 +689,17 @@
     sectors, doms = lax.axis_size("sector"), lax.axis_size("dom")
     out = jax.ShapeDtypeStruct(velocity.shape, jnp.float32)
     vmem = pl.BlockSpec(memory_space=pltpu.VMEM)
-    smem = pl.BlockSpec(memory_space=pltpu.SMEM)
     hbm = pl.BlockSpec(memory_space=pl.ANY)
     history = pltpu.VMEM((3, 8, 2 * LANES), jnp.float32)
+    small = pltpu.VMEM((doms, 2, LANES), jnp.float32)
     f32 = jnp.float32
     result = pl.pallas_call(
         functools.partial(kernel, sectors, doms),
         out_shape=pltpu.VMEM((8, 2 * LANES), f32),
-        in_specs=[hbm, hbm, smem] + [hbm] * 9,
+        in_specs=[hbm] * 12,
         out_specs=vmem,
         scratch_shapes=[
+            pltpu.SMEM(counts.shape, jnp.int32),
             pltpu.VMEM(strain_map.shape, f32),
             pltpu.VMEM(corner_nodes.shape, jnp.int32),
             pltpu.VMEM(velocity.shape, f32),
@@ -584,7 +715,15 @@
             pltpu.VMEM((8, LANES), f32),
             pltpu.VMEM((9, 8, LANES), f32),
             pltpu.VMEM(seam_nodes.shape, jnp.int32),
-            pltpu.VMEM((2, doms, 8, LANES), f32),
+            pltpu.VMEM(seam_nodes.shape, jnp.int32),
+            small,
+            small,
+            small,
+            small,
+            small,
+            small,
+            small,
+            pltpu.VMEM((1, doms, 8, LANES), f32),
             pltpu.VMEM((2, 2, 8, LANES), f32),
             pltpu.VMEM((2, doms + 2, 8, LANES), f32),
             pltpu.VMEM((2, doms, 8, LANES), f32),
@@ -598,9 +737,10 @@
             pltpu.VMEM((sectors, 1, LANES), f32),
             pltpu.VMEM((4 * doms, 8 * LANES), jnp.bfloat16),
             pltpu.VMEM((4 * doms + 16, 8 * LANES), jnp.bfloat16),
-            pltpu.SemaphoreType.DMA((10,)),
-            pltpu.SemaphoreType.DMA((18,)),
-            pltpu.SemaphoreType.DMA((18,)),
+            pltpu.SemaphoreType.DMA((12,)),
+            pltpu.SemaphoreType.REGULAR,
+            pltpu.SemaphoreType.DMA((21,)),
+            pltpu.SemaphoreType.DMA((21,)),
         ],
         compiler_params=pltpu.CompilerParams(collective_id=0, has_side_effects=True),
         name="dome",

time: 72.4 us -> 69.1 us (0.954)
  Pallas kernels: 69.8 us -> 66.5 us
    pallas_call x1, Pallas kernels: 69.8 us -> 66.5 us  [per_device(): pl.pallas_call(functools.partial(kernel, sectors, doms), out_shape=pltpu....]
where the time goes in v5:
time: 69.1 us; the launch traced here: 68.4 us
  Pallas kernels  66.5 us (96%)
  between operations  1.29 us (2%)
    pallas_call x1, Pallas kernels, per_device(): pl.pallas_call(functools.partial(kernel, sectors, doms), out_shape=pltpu....  66.5 us

profile of v5, /device:TPU:1, one launch (start us, length us, event | category | flops | bytes accessed | tf_op | source)
XLA Modules:
  0.0 68.4 jit_solution(299677100241381636)
XLA Ops:
  1.3 66.5 %dome.1 = f32[8,256]{1,0:T(8,128)S(1)} custom-call(f32[36,256]{1,0:T(8,128)} %strain_hbm.1, s32[4,256]{1,0:T(4,128)} %corner_hbm.1, s32[1]{0:T(128)S(6)} %copy.14.counts_hbm, s32[1,2048]{1,0:T(1,128)} %seam_hbm.1, f32[3,256]{1,0:T(4,128)} %velocity_hbm.1, f32[3,256]{1,0:T(4,128)} %dual_hbm.1, f32[3,256]{1,0:T(4,128)} %load_hbm.1, f32[2,128]{1,0:T(2,128)} %bitcast.9, ...), custom_call_target="tpu_custom_call" | custom-call | tf_op jit(solution)/shard_map/dome/pallas_call | solution.py:696
  67.8 0.6 fusion

commit v6 on v5

--- a/solution.py
+++ b/solution.py
@@ -86,6 +86,7 @@
     onehot,
     lhs_far,
     lhs_near,
+    lhs_own,
     gram_out,
     gram_in,
     total_out,
@@ -125,23 +126,10 @@
 
     chips = doms // 2
     reach = chips // 4
-    back, ahead = reach, reach
     chip, core = dom // 2, lax.rem(dom, 2)
 
     def at(offset, c):
         return 2 * lax.rem(chip + offset + chips, chips) + c
-
-    def greet_next(k, c):
-        signal(next_sec, at(k // 2 - reach, lax.rem(k, 2)))
-        return c
-
-    def greet_back(k, c):
-        signal(sec, at(k // 2 - back, lax.rem(k, 2)))
-        return c
-
-    def greet_ahead(k, c):
-        signal(sec, at(k // 2 + 1, lax.rem(k, 2)))
-        return c
 
     def greet_sec(o, c):
         signal(lax.rem(sec + o, sectors), dom)
@@ -167,9 +155,12 @@
         )
     ]
     loads[0].start()
-    lax.fori_loop(0, 2 * (2 * reach + 1), greet_next, 0)
-    lax.fori_loop(0, 2 * back, greet_back, 0)
-    lax.fori_loop(0, 2 * ahead, greet_ahead, 0)
+    for distance in range(reach, -1, -1):
+        for offset in sorted({distance, -distance}):
+            for c in range(2):
+                signal(next_sec, at(offset, c))
+                if distance > 0:
+                    signal(sec, at(offset, c))
     signal(sec, at(0, 1 - core))
     lax.fori_loop(2, sectors - 1, greet_sec, 0)
     for l in loads[1:]:
@@ -193,7 +184,7 @@
         jnp.broadcast_to(mobility[1:2, :], (8, LANES)),
     )
 
-    pl.semaphore_wait(barrier, 2 * (2 * reach + 1) + 2 * (back + ahead) + 1 + (sectors - 3))
+    pl.semaphore_wait(barrier, 2 * (2 * reach + 1) + 4 * reach + 1 + (sectors - 3))
 
     six = pl.ds(0, 6)
 
@@ -480,10 +471,10 @@
         split = [jnp.concatenate(p, axis=1) for p in split]
         split = [jnp.concatenate([p, p], axis=0).astype(jnp.bfloat16) for p in split]
 
-        def fill(lhs, mask):
-            for q in range(mask.shape[0] // 16):
+        def fill(lhs, mask, first=0):
+            for q in range(lhs.shape[1] // 16):
                 rows = slice(16 * q, 16 * q + 16)
-                hit = mask[rows, :]
+                hit = mask[first + 16 * q : first + 16 * q + 16, :]
                 for s in range(3):
                     lhs[s, rows, :] = hit * split[s]
 
@@ -501,21 +492,35 @@
             copy(force.at[it, k, six], force_in.at[it, dom, six], 10 + it, next_sec, far_first(k)).start()
             return c
 
-        fill(lhs_far, mask_far)
-        force[it, 0:half] = product(lhs_far)
-        if it == 1:
-            lax.fori_loop(0, half, send, 0)
-        fill(lhs_near, mask_near)
-        force[it, half : doms + 2] = product(lhs_near)
+        def send_pushes():
+            copy(force.at[it, doms, six], push_in.at[it, 1, six], 12 + 2 * it, sec, left).start()
+            copy(force.at[it, doms + 1, six], push_in.at[it, 0, six], 13 + 2 * it, sec, right).start()
+
+        def spread_own():
+            fill(lhs_own, mask_near, 4 * doms)
+            force[it, doms : doms + 2] = product(lhs_own)
+
+        def spread_half(lhs, mask, first):
+            fill(lhs, mask)
+            force[it, first : first + half] = product(lhs)
+
         if it == 0:
+            spread_own()
             own_forces()
             lax.fori_loop(0, doms, send_own, 0)
+            spread_half(lhs_far, mask_far, 0)
+            spread_half(lhs_near, mask_near, half)
             seam_forces()
             lax.fori_loop(0, doms - 1, send_seam, 0)
+            lax.fori_loop(0, doms, send, 0)
+            send_pushes()
+        else:
+            spread_half(lhs_far, mask_far, 0)
             lax.fori_loop(0, half, send, 0)
-        lax.fori_loop(half, doms, send, 0)
-        copy(force.at[it, doms, six], push_in.at[it, 1, six], 12 + 2 * it, sec, left).start()
-        copy(force.at[it, doms + 1, six], push_in.at[it, 0, six], 13 + 2 * it, sec, right).start()
+            spread_half(lhs_near, mask_near, half)
+            lax.fori_loop(half, doms, send, 0)
+            spread_own()
+            send_pushes()
 
     def next_speed(it):
         even = lax.rem(iota_row, 2) == 0
@@ -534,9 +539,9 @@
         return jnp.where(iota_row < 6, step, 0.0)
 
     wait_first()
+    dual_one, push = elements(0, dual_prev)
     pl.semaphore_wait(ready, 4)
     lax.fori_loop(0, doms, send_base, 0)
-    dual_one, push = elements(0, dual_prev)
     spread(0, push)
     collect()
     wait_force(0)
@@ -602,11 +607,11 @@
     total = add_all(gram_out[0], gram_in, 0, doms - 1)
     total_out[0] = total
 
-    def send_total(o, c):
+    def steps(o):
+        return min(o % 4, 4 - o % 4) + min(o // 4, sectors // 4 - o // 4)
+
+    for o in sorted(range(1, sectors), key=steps, reverse=True):
         copy(total_out.at[0], total_in.at[o], 17, lax.rem(sec + o, sectors), dom).start()
-        return c
-
-    lax.fori_loop(1, sectors, send_total, 0)
     block = total_in.at[pl.ds(1, sectors - 1)]
     total_copies = copy(block, block, 17, sec, dom)
 
@@ -730,7 +735,8 @@
             pltpu.VMEM((2, 2, 8, LANES), f32),
             pltpu.VMEM((LANES, 8 * LANES), jnp.bfloat16),
             pltpu.VMEM((3, 4 * doms, 8 * LANES), jnp.bfloat16),
-            pltpu.VMEM((3, 4 * doms + 16, 8 * LANES), jnp.bfloat16),
+            pltpu.VMEM((3, 4 * doms, 8 * LANES), jnp.bfloat16),
+            pltpu.VMEM((3, 16, 8 * LANES), jnp.bfloat16),
             pltpu.VMEM((1, 1, LANES), f32),
             pltpu.VMEM((doms, 1, LANES), f32),
             pltpu.VMEM((1, 1, LANES), f32),

time: 69.1 us -> 68 us (0.984)
  Pallas kernels: 66.5 us -> 65.6 us
    pallas_call x1, Pallas kernels: 66.5 us -> 65.6 us  [per_device(): pl.pallas_call(functools.partial(kernel, sectors, doms), out_shape=pltpu....]
where the time goes in v6:
time: 68 us; the launch traced here: 67.5 us
  Pallas kernels  65.6 us (96%)
  between operations  1.29 us (2%)
    pallas_call x1, Pallas kernels, per_device(): pl.pallas_call(functools.partial(kernel, sectors, doms), out_shape=pltpu....  65.6 us

profile of v6, /device:TPU:1, one launch (start us, length us, event | category | flops | bytes accessed | tf_op | source)
XLA Modules:
  0.0 67.5 jit_solution(5419549390963642372)
XLA Ops:
  1.3 65.6 %dome.1 = f32[8,256]{1,0:T(8,128)S(1)} custom-call(f32[36,256]{1,0:T(8,128)} %strain_hbm.1, s32[4,256]{1,0:T(4,128)} %corner_hbm.1, s32[1]{0:T(128)S(6)} %copy.14.counts_hbm, s32[1,2048]{1,0:T(1,128)} %seam_hbm.1, f32[3,256]{1,0:T(4,128)} %velocity_hbm.1, f32[3,256]{1,0:T(4,128)} %dual_hbm.1, f32[3,256]{1,0:T(4,128)} %load_hbm.1, f32[2,128]{1,0:T(2,128)} %bitcast.9, ...), custom_call_target="tpu_custom_call" | custom-call | tf_op jit(solution)/shard_map/dome/pallas_call | solution.py:701
  66.9 0.6 fusion

commit v7 on v6

--- a/solution.py
+++ b/solution.py
@@ -515,8 +515,12 @@
             lax.fori_loop(0, doms, send, 0)
             send_pushes()
         else:
-            spread_half(lhs_far, mask_far, 0)
-            lax.fori_loop(0, half, send, 0)
+            quarter = half // 2
+            for q in range(2):
+                rows = pl.ds(8 * quarter * q, 8 * quarter)
+                fill(lhs_far.at[:, rows], mask_far, 8 * quarter * q)
+                force[it, quarter * q : quarter * (q + 1)] = product(lhs_far.at[:, rows])
+                lax.fori_loop(quarter * q, quarter * (q + 1), send, 0)
             spread_half(lhs_near, mask_near, half)
             lax.fori_loop(half, doms, send, 0)
             spread_own()
@@ -538,10 +542,11 @@
         step = speed[it] - mob6[...] * (own - load6[...])
         return jnp.where(iota_row < 6, step, 0.0)
 
+    lax.fori_loop(half, doms, send_base, 0)
     wait_first()
     dual_one, push = elements(0, dual_prev)
     pl.semaphore_wait(ready, 4)
-    lax.fori_loop(0, doms, send_base, 0)
+    lax.fori_loop(0, half, send_base, 0)
     spread(0, push)
     collect()
     wait_force(0)

time: 68 us -> 67.6 us (level)
  no operation moved by 1% of the time
where the time goes in v7:
time: 67.6 us; the launch traced here: 67 us
  Pallas kernels  65.2 us (96%)
  between operations  1.29 us (2%)
    pallas_call x1, Pallas kernels, per_device(): pl.pallas_call(functools.partial(kernel, sectors, doms), out_shape=pltpu....  65.2 us

profile of v7, /device:TPU:1, one launch (start us, length us, event | category | flops | bytes accessed | tf_op | source)
XLA Modules:
  0.0 67.0 jit_solution(13166706552585314225)
XLA Ops:
  1.3 65.2 %dome.1 = f32[8,256]{1,0:T(8,128)S(1)} custom-call(f32[36,256]{1,0:T(8,128)} %strain_hbm.1, s32[4,256]{1,0:T(4,128)} %corner_hbm.1, s32[1]{0:T(128)S(6)} %copy.14.counts_hbm, s32[1,2048]{1,0:T(1,128)} %seam_hbm.1, f32[3,256]{1,0:T(4,128)} %velocity_hbm.1, f32[3,256]{1,0:T(4,128)} %dual_hbm.1, f32[3,256]{1,0:T(4,128)} %load_hbm.1, f32[2,128]{1,0:T(2,128)} %bitcast.9, ...), custom_call_target="tpu_custom_call" | custom-call | tf_op jit(solution)/shard_map/dome/pallas_call | solution.py:706
  66.4 0.6 fusion
